TPU v7x, 768 devices: a whole 4x8x12 slice. The times are simulated.
768 devices in a mesh: grp: 24 (over z, core), seg: 32 (over y, x).
Axes of the slice: x: 4, y: 8, z: 12, core: 2. Of those that a mesh axis runs over, the one named last changes fastest.
Arguments:
- initial_field: float32 [4, 96, 1024, 32], P(None, 'grp', 'seg'), may hold values from -6 to 6
- base_reluctivity: float32 [96, 1024, 32], P('grp', 'seg'), may hold values from 0.85 to 1
- saturation_rate: float32 [96, 1024, 32], P('grp', 'seg'), may hold values from 1 to 5
- mixing: float32 [4, 4], replicated, may hold values from -3 to 3
- face_contact: int32 [24, 256, 6], P('grp', 'seg'), may hold values 0 or 1
- new_owner: int32 [24, 256], P('grp', 'seg'), may hold values from 0 to 31, as said below
Outputs:
- new_blocks: float32 [24576, 4, 4, 128], P(('grp', 'seg'))
Inputs may be any that keep to these rules, and one draw needn't show every extreme that they name: `new_owner`: of the blocks of one old owner, at most 1 go to the same new owner. In every group one new owner receives exactly 1 block from every old owner of the group, so exactly 32 blocks; the others receive fewer.
All inputs are finite; a program needn't handle non-finite values. No bound on the sum of `face_contact` on one device may be relied on, other than what follows from the above.
Results may differ from a plain program's by a relative error of at most 0.00007.
Values sent between devices are 32-bit elements; how exact they have to be, the bound alone decides.
No kernel may reach another device: no remote copies, remote signals or barrier semaphores. Data moves between devices by JAX's collectives and lax.ppermute only.
A program may use at most 32 MiB of HBM per device.

v0:
```python
import jax
import jax.numpy as jnp
from jax import lax
from jax.sharding import PartitionSpec as P

BXC = 4
BYC = 16
BZC = 8
BLY = 2
BLZ = 4
SLOT = 1
STEPS1 = 4
STEPS2 = 4


step_size = 0.05


def with_halo(array, sides, width):
    for axis, dim in sides:
        size, length = (lax.axis_size(axis), array.shape[dim])
        up = [(i, (i + 1) % size) for i in range(size - 1)]
        down = [(j, i) for i, j in up]
        last = lax.slice_in_dim(array, length - width, length, axis=dim)
        leading = lax.slice_in_dim(array, 0, width, axis=dim)
        before = lax.ppermute(last, axis, up)
        after = lax.ppermute(leading, axis, down)
        array = jnp.concatenate([before, array, after], axis=dim)
    return array


def advance(components, neighbours, coefficients, base_reluctivity, saturation_rate, mixing):
    differences = [
        [
            coefficients[direction] * (neighbours[direction][channel] - components[channel])
            for channel in range(4)
        ]
        for direction in range(6)
    ]
    field_x = differences[3][2] - differences[5][1]
    field_y = differences[5][0] - differences[1][2]
    field_z = differences[1][1] - differences[3][0]
    saturation = saturation_rate * (field_x * field_x + field_y * field_y + field_z * field_z)
    reluctivity = base_reluctivity * (1.0 + 2.0 * saturation / (1.0 + saturation))
    updated = []
    for channel in range(4):
        laplacian = differences[0][channel]
        for direction in range(1, 6):
            laplacian = laplacian + differences[direction][channel]
        coupled = mixing[channel, 0] * components[0]
        for source_channel in range(1, 4):
            coupled = coupled + mixing[channel, source_channel] * components[source_channel]
        updated.append(components[channel] + step_size * (reluctivity * laplacian + coupled))
    return updated


def slab_coefficients(grid):
    blocks_x, blocks_y, blocks_z = (grid.shape[0], grid.shape[1], grid.shape[2])
    position_x = (jnp.arange(blocks_x * BXC) % BXC)[:, None, None]
    position_y = (jnp.arange(blocks_y * BYC) % BYC)[None, :, None]
    position_z = (jnp.arange(blocks_z * BZC) % BZC)[None, None, :]
    edge_cells = [
        position_x == 0,
        position_x == BXC - 1,
        position_y == 0,
        position_y == BYC - 1,
        position_z == 0,
        position_z == BZC - 1,
    ]
    result = []
    for direction in range(6):
        spread = grid[:, :, :, direction].astype(jnp.float32)
        spread = jnp.repeat(jnp.repeat(jnp.repeat(spread, BXC, axis=0), BYC, axis=1), BZC, axis=2)
        result.append(jnp.where(edge_cells[direction], spread, jnp.ones_like(spread)))
    return result


def slab_step(state, padded, coefficients, base_reluctivity, saturation_rate, mixing):
    neighbours = [
        padded[:, :-2, 1:-1, 1:-1],
        padded[:, 2:, 1:-1, 1:-1],
        padded[:, 1:-1, :-2, 1:-1],
        padded[:, 1:-1, 2:, 1:-1],
        padded[:, 1:-1, 1:-1, :-2],
        padded[:, 1:-1, 1:-1, 2:],
    ]
    return jnp.stack(
        advance(state, neighbours, coefficients, base_reluctivity, saturation_rate, mixing)
    )


def block_coefficients():
    position_x = jnp.arange(BXC)[:, None]
    merged = jnp.arange(BYC * BZC)[None, :]
    position_y = merged // BZC
    position_z = merged % BZC
    tests = [
        position_x > 0,
        position_x < BXC - 1,
        position_y > 0,
        position_y < BYC - 1,
        position_z > 0,
        position_z < BZC - 1,
    ]
    return [jnp.where(test, 1.0, 0.0).astype(jnp.float32) for test in tests]


def block_steps(blocks, material, mixing):
    state = jnp.moveaxis(blocks, 1, 0)
    properties = jnp.moveaxis(material, 1, 0)
    coefficients = block_coefficients()
    for sweep in range(STEPS2):
        neighbours = [
            jnp.roll(state, 1, 2),
            jnp.roll(state, -1, 2),
            jnp.roll(state, BZC, 3),
            jnp.roll(state, -BZC, 3),
            jnp.roll(state, 1, 3),
            jnp.roll(state, -1, 3),
        ]
        state = jnp.stack(
            advance(state, neighbours, coefficients, properties[0], properties[1], mixing)
        )
    return jnp.moveaxis(state, 0, 1)


def to_blocks(array):
    channels = array.shape[0]
    blocks_x = array.shape[1] // BXC
    blocks_y = array.shape[2] // BYC
    blocks_z = array.shape[3] // BZC
    shaped = array.reshape(channels, blocks_x, BXC, blocks_y, BYC, blocks_z, BZC)
    shaped = shaped.transpose(1, 3, 5, 0, 2, 4, 6)
    return shaped.reshape(blocks_x * blocks_y * blocks_z, channels, BXC, BYC * BZC)


def slot_rank(owners):
    count = owners.shape[-1]
    same = owners[..., :, None] == owners[..., None, :]
    earlier = jnp.arange(count)[None, :] < jnp.arange(count)[:, None]
    return jnp.sum(jnp.logical_and(same, earlier), axis=-1)


def surround(state):
    padded = with_halo(state, (("grp", 1), ("seg", 2)), 1)
    return jnp.pad(padded, ((0, 0), (0, 0), (0, 0), (1, 1)))


def on_device(initial_field, base_reluctivity, saturation_rate, mixing, face_contact, new_owner):
    coefficients = slab_coefficients(face_contact[0].reshape(1, BLY, BLZ, 6))
    state = initial_field
    for sweep in range(STEPS1):
        state = slab_step(
            state, surround(state), coefficients, base_reluctivity, saturation_rate, mixing
        )
    blocks = to_blocks(state)
    material = to_blocks(jnp.stack([base_reluctivity, saturation_rate]))
    owners = new_owner[0]
    ranks = slot_rank(owners)
    peers = lax.axis_size("seg")
    slots = peers * SLOT
    target = owners * SLOT + ranks
    selector = (target[None, :] == jnp.arange(slots)[:, None]).astype(jnp.float32)

    def pack(array):
        placed = jnp.einsum("sb,bcxm->scxm", selector, array, precision=lax.Precision.HIGHEST)
        return placed.reshape(peers, SLOT, array.shape[1], BXC, BYC * BZC)

    field_part = lax.all_to_all(pack(blocks), "seg", split_axis=0, concat_axis=0, tiled=True)
    material_part = lax.all_to_all(pack(material), "seg", split_axis=0, concat_axis=0, tiled=True)
    done = block_steps(
        field_part.reshape(-1, 4, BXC, BYC * BZC),
        material_part.reshape(-1, 2, BXC, BYC * BZC),
        mixing,
    )
    received = done.reshape(field_part.shape)
    return received.reshape(slots, 4, BXC, BYC * BZC)


def solution(mesh):
    return jax.shard_map(
        on_device,
        mesh=mesh,
        in_specs=(
            P(None, "grp", "seg", None),
            P("grp", "seg", None),
            P("grp", "seg", None),
            P(),
            P("grp", "seg", None),
            P("grp", "seg"),
        ),
        out_specs=P(("grp", "seg"), None, None, None),
        check_vma=False,
    )
```

profile of v0, /device:TPU:193, one launch (start us, length us, event | category | flops | bytes accessed | tf_op | source)
XLA Modules:
  0.0 203.5 jit_solution(15206883149243438320)
XLA Ops:
  3.5 5.2 %collective-permute-start = (f32[4,1,32,32]{3,2,1,0:T(8,128)S(1)}, f32[4,1,32,32]{3,2,1,0:T(8,128)S(1)}, u32[]{:S(2)}, u32[]{:S(2)}) collective-permute-start(f32[4,1,32,32]{3,2,1,0:T(8,128)S(1)} %get-tuple-element.85), channel_id=1, source_target_pairs={{0,32},{32,64},{64,96},{96,128},{128,160},{160,192},{192,224},{224... | collective-permute-start | bytes 49160 | tf_op jit(solution)/shard_map/ppermute | solution.py:26
  11.5 3.1 %collective-permute-start.3 = (f32[4,6,1,32]{3,2,1,0:T(1,128)S(1)}, f32[4,6,1,32]{3,2,1,0:T(1,128)S(1)}, u32[]{:S(2)}, u32[]{:S(2)}) collective-permute-start(f32[4,6,1,32]{3,2,1,0:T(1,128)S(1)} %get-tuple-element.23), channel_id=1, source_target_pairs={{0,1},{1,2},{2,3},{3,4},{4,5},{5,6},{6,7},{7,8},{8,9},{9,10},{10,1... | collective-permute-start | bytes 9224 | tf_op jit(solution)/shard_map/ppermute | solution.py:26
  16.4 2.7 %collective-permute-done.2 = f32[4,6,1,32]{3,2,1,0:T(1,128)S(1)} collective-permute-done((f32[4,6,1,32]{3,2,1,0:T(1,128)S(1)}, f32[4,6,1,32]{3,2,1,0:T(1,128)S(1)}, u32[]{:S(2)}, u32[]{:S(2)}) %collective-permute-start.2) | collective-permute-done | bytes 3104 | tf_op jit(solution)/shard_map/ppermute | solution.py:27
  19.9 2.7 %fusion.457 = f32[4,32,32]{2,1,0:T(8,128)S(1)} fusion(f32[4,6,34,34]{3,2,1,0:T(8,128)S(1)} %select_maximum_fusion, f32[4,6,32,32]{3,2,1,0:T(8,128)S(1)} %get-tuple-element.89, f32[4,6,1,32]{3,2,1,0:T(1,128)S(1)} %collective-permute-done.3, f32[4,5,32,32]{3,2,1,0:T(8,128)S(1)} %get-tuple-element.88, f32[4,5,32,32]{3,2,1,0:T(8,128)S(1)} %get-tuple-element.81, ...), kind=kLoop, calls=%fused_computation.738 | loop fusion | flops 241664 | bytes 358552 | tf_op jit(solution)/shard_map/add | solution.py:53
  22.7 2.8 %fusion.379 = f32[4,32,32]{2,1,0:T(8,128)S(1)} fusion(f32[4,6,34,34]{3,2,1,0:T(8,128)S(1)} %select_maximum_fusion, f32[4,6,1,32]{3,2,1,0:T(1,128)S(1)} %collective-permute-done.2, f32[4,6,32,32]{3,2,1,0:T(8,128)S(1)} %get-tuple-element.89, f32[4,6,1,32]{3,2,1,0:T(1,128)S(1)} %collective-permute-done.3, f32[4,5,32,32]{3,2,1,0:T(8,128)S(1)} %get-tuple-element.81, ...), kind=kLoop, calls=%fused_computation.660 | loop fusion | flops 245760 | bytes 342168 | tf_op jit(solution)/shard_map/add | solution.py:53
  30.7 5.6 %collective-permute-start.4 = (f32[4,1,32,32]{3,2,1,0:T(8,128)S(1)}, f32[4,1,32,32]{3,2,1,0:T(8,128)S(1)}, u32[]{:S(2)}, u32[]{:S(2)}) collective-permute-start(f32[4,1,32,32]{3,2,1,0:T(8,128)S(1)} %get-tuple-element.79), channel_id=1, source_target_pairs={{0,32},{32,64},{64,96},{96,128},{128,160},{160,192},{192,224},{224... | collective-permute-start | bytes 49160 | tf_op jit(solution)/shard_map/ppermute | solution.py:26
  38.3 4.9 %collective-permute-done.5 = f32[4,1,32,32]{3,2,1,0:T(8,128)S(1)} collective-permute-done((f32[4,1,32,32]{3,2,1,0:T(8,128)S(1)}, f32[4,1,32,32]{3,2,1,0:T(8,128)S(1)}, u32[]{:S(2)}, u32[]{:S(2)}) %collective-permute-start.5) | collective-permute-done | bytes 16416 | tf_op jit(solution)/shard_map/ppermute | solution.py:27
  43.2 3.1 %collective-permute-start.7 = (f32[4,6,1,32]{3,2,1,0:T(1,128)S(1)}, f32[4,6,1,32]{3,2,1,0:T(1,128)S(1)}, u32[]{:S(2)}, u32[]{:S(2)}) collective-permute-start(f32[4,6,1,32]{3,2,1,0:T(1,128)S(1)} %get-tuple-element.21), channel_id=1, source_target_pairs={{0,1},{1,2},{2,3},{3,4},{4,5},{5,6},{6,7},{7,8},{8,9},{9,10},{10,1... | collective-permute-start | bytes 9224 | tf_op jit(solution)/shard_map/ppermute | solution.py:26
  47.6 3.1 %collective-permute-done.6 = f32[4,6,1,32]{3,2,1,0:T(1,128)S(1)} collective-permute-done((f32[4,6,1,32]{3,2,1,0:T(1,128)S(1)}, f32[4,6,1,32]{3,2,1,0:T(1,128)S(1)}, u32[]{:S(2)}, u32[]{:S(2)}) %collective-permute-start.6) | collective-permute-done | bytes 3104 | tf_op jit(solution)/shard_map/ppermute | solution.py:27
  53.4 2.7 %fusion.468 = f32[4,32,32]{2,1,0:T(8,128)S(1)} fusion(f32[4,32,32]{2,1,0:T(8,128)S(1)} %fusion.457, f32[4,6,34,32]{3,2,1,0:T(8,128)S(1)} %pad_maximum_fusion, f32[4,6,1,32]{3,2,1,0:T(1,128)S(1)} %collective-permute-done.7, f32[4,1,32,32]{3,2,1,0:T(8,128)S(1)} %collective-permute-done.5, f32[4,1,32,32]{3,2,1,0:T(8,128)S(1)} %collective-permute-done.4, ...), kind=kLoop, calls=%fused_computation.749 | loop fusion | flops 368640 | bytes 348312 | tf_op jit(solution)/shard_map/add | solution.py:53
  58.8 2.8 %fusion.393 = f32[4,32,32]{2,1,0:T(8,128)S(1)} fusion(f32[4,32,32]{2,1,0:T(8,128)S(1)} %fusion.379, f32[4,6,34,32]{3,2,1,0:T(8,128)S(1)} %pad_maximum_fusion, f32[4,6,1,32]{3,2,1,0:T(1,128)S(1)} %collective-permute-done.6, f32[4,1,32,32]{3,2,1,0:T(8,128)S(1)} %collective-permute-done.5, f32[4,1,32,32]{3,2,1,0:T(8,128)S(1)} %collective-permute-done.4, ...), kind=kLoop, calls=%fused_computation.674 | loop fusion | flops 376832 | bytes 348312 | tf_op jit(solution)/shard_map/add | solution.py:53
  61.6 3.3 %collective-permute-start.8 = (f32[4,1,32,32]{3,2,1,0:T(8,128)S(1)}, f32[4,1,32,32]{3,2,1,0:T(8,128)S(1)}, u32[]{:S(2)}, u32[]{:S(2)}) collective-permute-start(f32[4,1,32,32]{3,2,1,0:T(8,128)S(1)} %get-tuple-element.77), channel_id=1, source_target_pairs={{0,32},{32,64},{64,96},{96,128},{128,160},{160,192},{192,224},{224... | collective-permute-start | bytes 49160 | tf_op jit(solution)/shard_map/ppermute | solution.py:26
  67.0 4.7 %collective-permute-done.9 = f32[4,1,32,32]{3,2,1,0:T(8,128)S(1)} collective-permute-done((f32[4,1,32,32]{3,2,1,0:T(8,128)S(1)}, f32[4,1,32,32]{3,2,1,0:T(8,128)S(1)}, u32[]{:S(2)}, u32[]{:S(2)}) %collective-permute-start.9) | collective-permute-done | bytes 16416 | tf_op jit(solution)/shard_map/ppermute | solution.py:27
  71.7 4.4 %collective-permute-start.11 = (f32[4,6,1,32]{3,2,1,0:T(1,128)S(1)}, f32[4,6,1,32]{3,2,1,0:T(1,128)S(1)}, u32[]{:S(2)}, u32[]{:S(2)}) collective-permute-start(f32[4,6,1,32]{3,2,1,0:T(1,128)S(1)} %get-tuple-element.19), channel_id=1, source_target_pairs={{0,1},{1,2},{2,3},{3,4},{4,5},{5,6},{6,7},{7,8},{8,9},{9,10},{10,1... | collective-permute-start | bytes 9224 | tf_op jit(solution)/shard_map/ppermute | solution.py:26
  77.9 3.0 %collective-permute-done.10 = f32[4,6,1,32]{3,2,1,0:T(1,128)S(1)} collective-permute-done((f32[4,6,1,32]{3,2,1,0:T(1,128)S(1)}, f32[4,6,1,32]{3,2,1,0:T(1,128)S(1)}, u32[]{:S(2)}, u32[]{:S(2)}) %collective-permute-start.10) | collective-permute-done | bytes 3104 | tf_op jit(solution)/shard_map/ppermute | solution.py:27
  83.5 2.7 %fusion.479 = f32[4,32,32]{2,1,0:T(8,128)S(1)} fusion(f32[4,32,32]{2,1,0:T(8,128)S(1)} %fusion.468, f32[4,6,34,32]{3,2,1,0:T(8,128)S(1)} %pad_maximum_fusion.1, f32[4,6,1,32]{3,2,1,0:T(1,128)S(1)} %collective-permute-done.11, f32[4,1,32,32]{3,2,1,0:T(8,128)S(1)} %collective-permute-done.9, f32[4,1,32,32]{3,2,1,0:T(8,128)S(1)} %collective-permute-done.8, ...), kind=kLoop, calls=%fused_computation.760 | loop fusion | flops 368640 | bytes 348312 | tf_op jit(solution)/shard_map/add | solution.py:53
  88.9 2.8 %fusion.407 = f32[4,32,32]{2,1,0:T(8,128)S(1)} fusion(f32[4,32,32]{2,1,0:T(8,128)S(1)} %fusion.393, f32[4,6,34,32]{3,2,1,0:T(8,128)S(1)} %pad_maximum_fusion.1, f32[4,6,1,32]{3,2,1,0:T(1,128)S(1)} %collective-permute-done.10, f32[4,1,32,32]{3,2,1,0:T(8,128)S(1)} %collective-permute-done.9, f32[4,1,32,32]{3,2,1,0:T(8,128)S(1)} %collective-permute-done.8, ...), kind=kLoop, calls=%fused_computation.688 | loop fusion | flops 376832 | bytes 348312 | tf_op jit(solution)/shard_map/add | solution.py:53
  91.7 3.0 %collective-permute-start.12 = (f32[4,1,32,32]{3,2,1,0:T(8,128)S(1)}, f32[4,1,32,32]{3,2,1,0:T(8,128)S(1)}, u32[]{:S(2)}, u32[]{:S(2)}) collective-permute-start(f32[4,1,32,32]{3,2,1,0:T(8,128)S(1)} %get-tuple-element.75), channel_id=1, source_target_pairs={{0,32},{32,64},{64,96},{96,128},{128,160},{160,192},{192,224},{224... | collective-permute-start | bytes 49160 | tf_op jit(solution)/shard_map/ppermute | solution.py:26
  97.3 4.2 %collective-permute-done.13 = f32[4,1,32,32]{3,2,1,0:T(8,128)S(1)} collective-permute-done((f32[4,1,32,32]{3,2,1,0:T(8,128)S(1)}, f32[4,1,32,32]{3,2,1,0:T(8,128)S(1)}, u32[]{:S(2)}, u32[]{:S(2)}) %collective-permute-start.13) | collective-permute-done | bytes 16416 | tf_op jit(solution)/shard_map/ppermute | solution.py:27
  101.5 3.7 %collective-permute-start.15 = (f32[4,6,1,32]{3,2,1,0:T(1,128)S(1)}, f32[4,6,1,32]{3,2,1,0:T(1,128)S(1)}, u32[]{:S(2)}, u32[]{:S(2)}) collective-permute-start(f32[4,6,1,32]{3,2,1,0:T(1,128)S(1)} %get-tuple-element.17), channel_id=1, source_target_pairs={{0,1},{1,2},{2,3},{3,4},{4,5},{5,6},{6,7},{7,8},{8,9},{9,10},{10,1... | collective-permute-start | bytes 9224 | tf_op jit(solution)/shard_map/ppermute | solution.py:26
  107.7 15.3 %all-to-all-start.1 = ((f32[32,1,2,4,128]{4,3,2,1,0:T(4,128)}), f32[32,1,2,4,128]{4,3,2,1,0:T(4,128)S(1)}, u32[]{:S(2)}, u32[]{:S(2)}) async-start(f32[32,1,2,4,128]{4,3,2,1,0:T(4,128)} %copy.118), calls=%async_computation.1 | async-start | bytes 262144 | tf_op jit(solution)/shard_map/all_to_all | solution.py:170
  125.7 2.7 %fusion.490 = f32[4,32,32]{2,1,0:T(8,128)S(1)} fusion(f32[4,32,32]{2,1,0:T(8,128)S(1)} %fusion.479, f32[4,6,34,32]{3,2,1,0:T(8,128)S(1)} %pad_maximum_fusion.2, f32[4,6,1,32]{3,2,1,0:T(1,128)S(1)} %collective-permute-done.15, f32[4,1,32,32]{3,2,1,0:T(8,128)S(1)} %collective-permute-done.13, f32[4,1,32,32]{3,2,1,0:T(8,128)S(1)} %collective-permute-done.12, ...), kind=kLoop, calls=%fused_computation.771 | loop fusion | flops 368640 | bytes 348312 | tf_op jit(solution)/shard_map/add | solution.py:53
  131.0 2.8 %fusion.421 = f32[4,32,32]{2,1,0:T(8,128)S(1)} fusion(f32[4,32,32]{2,1,0:T(8,128)S(1)} %fusion.407, f32[4,6,34,32]{3,2,1,0:T(8,128)S(1)} %pad_maximum_fusion.2, f32[4,6,1,32]{3,2,1,0:T(1,128)S(1)} %collective-permute-done.14, f32[4,1,32,32]{3,2,1,0:T(8,128)S(1)} %collective-permute-done.13, f32[4,1,32,32]{3,2,1,0:T(8,128)S(1)} %collective-permute-done.12, ...), kind=kLoop, calls=%fused_computation.702 | loop fusion | flops 376832 | bytes 348312 | tf_op jit(solution)/shard_map/add | solution.py:53
  137.1 9.4 %all-to-all-start = ((f32[32,1,4,4,128]{4,3,2,1,0:T(4,128)}), f32[32,1,4,4,128]{4,3,2,1,0:T(4,128)S(1)}, u32[]{:S(2)}, u32[]{:S(2)}) async-start(f32[32,1,4,4,128]{4,3,2,1,0:T(4,128)} %copy.113), calls=%async_computation | async-start | bytes 524288 | tf_op jit(solution)/shard_map/all_to_all | solution.py:169
  146.6 10.9 %all-to-all-done = f32[32,1,4,4,128]{4,3,2,1,0:T(4,128)S(1)} async-done(((f32[32,1,4,4,128]{4,3,2,1,0:T(4,128)}), f32[32,1,4,4,128]{4,3,2,1,0:T(4,128)S(1)}, u32[]{:S(2)}, u32[]{:S(2)}) %all-to-all-start) | async-done | bytes 262176 | tf_op jit(solution)/shard_map/all_to_all | solution.py:169
  158.4 2.8 %fusion.207 = (f32[1,32,4,128]{3,1,2,0:T(8,128)S(1)}, f32[1,32,4,128]{3,1,2,0:T(8,128)S(1)}, f32[1,32,4,128]{3,1,2,0:T(8,128)S(1)}, f32[1,32,4,128]{3,1,2,0:T(8,...) fusion(f32[1,32,4,128]{3,1,2,0:T(8,128)S(1)} %get-tuple-element.66, ...), kind=kLoop, calls=%fused_computation.488 | loop fusion | flops 884736 | bytes 2492464 | tf_op jit(solution)/shard_map/add | solution.py:53
  169.5 2.8 %fusion.147 = (f32[1,32,4,128]{3,1,2,0:T(8,128)S(1)}, f32[1,32,4,128]{3,1,2,0:T(8,128)S(1)}) fusion(f32[1,32,4,128]{3,1,2,0:T(8,128)S(1)} %get-tuple-element.11, f32[4,32,4,1]{3,1,2,0:T(8,128)S(1)} %get-tuple-element.56, f32[4,32,4,127]{3,1,2,0:T(8,128)S(1)} %get-tuple-element.54, f32[4,32,4,8]{3,1,2,0:T(8,128)S(1)} %get-tuple-element.58, ...), kind=kLoop, calls=%fused_computation.428 | loop fusion | flops 1081344 | bytes 2099248 | tf_op jit(solution)/shard_map/add | solution.py:53
  177.5 2.7 %fusion.138 = f32[1,32,4,128]{3,1,2,0:T(8,128)S(1)} fusion(f32[1,32,4,128]{3,1,2,0:T(8,128)S(1)} %fusion.198, f32[1,32,4,128]{3,1,2,0:T(8,128)S(1)} %get-tuple-element.10, f32[4,32,4,1]{3,1,2,0:T(8,128)S(1)} %get-tuple-element.56, f32[4,32,4,127]{3,1,2,0:T(8,128)S(1)} %get-tuple-element.54, f32[4,32,4,8]{3,1,2,0:T(8,128)S(1)} %get-tuple-element.58, ...), kind=kLoop, calls=%fused_computation.419 | loop fusion | flops 557056 | bytes 1968176 | tf_op jit(solution)/shard_map/add | solution.py:53
  180.8 2.8 %fusion.87 = (f32[1,32,4,128]{3,1,2,0:T(8,128)S(1)}, f32[1,32,4,128]{3,1,2,0:T(8,128)S(1)}) fusion(f32[1,32,4,128]{3,1,2,0:T(8,128)S(1)} %get-tuple-element.9, f32[4,32,4,1]{3,1,2,0:T(8,128)S(1)} %get-tuple-element.44, f32[4,32,4,127]{3,1,2,0:T(8,128)S(1)} %get-tuple-element.42, f32[4,32,4,8]{3,1,2,0:T(8,128)S(1)} %get-tuple-element.46, ...), kind=kLoop, calls=%fused_computation.368 | loop fusion | flops 1081344 | bytes 2099248 | tf_op jit(solution)/shard_map/add | solution.py:53
  188.7 2.7 %fusion.78 = f32[1,32,4,128]{3,1,2,0:T(8,128)S(1)} fusion(f32[1,32,4,128]{3,1,2,0:T(8,128)S(1)} %fusion.138, f32[1,32,4,128]{3,1,2,0:T(8,128)S(1)} %get-tuple-element.8, f32[4,32,4,1]{3,1,2,0:T(8,128)S(1)} %get-tuple-element.44, f32[4,32,4,127]{3,1,2,0:T(8,128)S(1)} %get-tuple-element.42, f32[4,32,4,8]{3,1,2,0:T(8,128)S(1)} %get-tuple-element.46, ...), kind=kLoop, calls=%fused_computation.359 | loop fusion | flops 557056 | bytes 1968176 | tf_op jit(solution)/shard_map/add | solution.py:53
  192.0 2.8 %fusion.18 = (f32[1,32,4,128]{3,1,2,0:T(8,128)S(1)}, f32[1,32,4,128]{3,1,2,0:T(8,128)S(1)}) fusion(f32[1,32,4,128]{3,1,2,0:T(8,128)S(1)} %fusion.78, f32[4,32,4,1]{3,1,2,0:T(8,128)S(1)} %get-tuple-element.28, f32[4,32,4,127]{3,1,2,0:T(8,128)S(1)} %get-tuple-element.26, f32[4,32,4,8]{3,1,2,0:T(8,128)S(1)} %get-tuple-element.32, ...), kind=kLoop, calls=%fused_computation.299 | loop fusion | flops 1081344 | bytes 2099248 | tf_op jit(solution)/shard_map/add | solution.py:53
  197.3 2.7 %fusion.27 = f32[1,32,4,128]{3,1,2,0:T(8,128)S(1)} fusion(f32[1,32,4,128]{3,1,2,0:T(8,128)S(1)} %get-tuple-element.7, f32[1,32,4,128]{3,1,2,0:T(8,128)S(1)} %get-tuple-element.6, f32[4,32,4,1]{3,1,2,0:T(8,128)S(1)} %get-tuple-element.28, f32[4,32,4,127]{3,1,2,0:T(8,128)S(1)} %get-tuple-element.26, f32[4,32,4,8]{3,1,2,0:T(8,128)S(1)} %get-tuple-element.32, ...), kind=kLoop, calls=%fused_computation.308 | loop fusion | flops 557056 | bytes 1968176 | tf_op jit(solution)/shard_map/add | solution.py:53
  (158 shorter events, 71.8 us)
Async XLA Ops:
  0.9 7.9 %copy-start.4 = (s32[1,8,6]{1,0,2:T(1,128)S(1)}, s32[1,8,6]{1,0,2:T(1,128)}, u32[]{:S(2)}) copy-start(s32[1,8,6]{1,0,2:T(1,128)} %param.10) | copy-start | bytes 580
  0.9 8.0 %copy-start.3 = (f32[4,4]{1,0:T(4,128)S(1)}, f32[4,4]{1,0:T(4,128)}, u32[]{:S(2)}) copy-start(f32[4,4]{1,0:T(4,128)} %param.9) | copy-start | bytes 196
  0.9 10.5 %collective-permute-start.1 = (f32[4,1,32,32]{3,2,1,0:T(8,128)S(1)}, f32[4,1,32,32]{3,2,1,0:T(8,128)S(1)}, u32[]{:S(2)}, u32[]{:S(2)}) collective-permute-start(f32[4,1,32,32]{3,2,1,0:T(8,128)S(1)} %get-tuple-element.84), channel_id=1, source_target_pairs={{32,0},{64,32},{96,64},{128,96},{160,128},{192,160},{224,192},{256... | collective-permute-start | bytes 49160 | tf_op jit(solution)/shard_map/ppermute | solution.py:27
  3.5 7.9 %copy-start.2 = (f32[4,4,32,32]{3,2,1,0:T(8,128)S(1)}, f32[4,4,32,32]{3,2,1,0:T(8,128)}, u32[]{:S(2)}) copy-start(f32[4,4,32,32]{3,2,1,0:T(8,128)} %param.6) | copy-start | bytes 196612
  3.5 7.8 %collective-permute-start = (f32[4,1,32,32]{3,2,1,0:T(8,128)S(1)}, f32[4,1,32,32]{3,2,1,0:T(8,128)S(1)}, u32[]{:S(2)}, u32[]{:S(2)}) collective-permute-start(f32[4,1,32,32]{3,2,1,0:T(8,128)S(1)} %get-tuple-element.85), channel_id=1, source_target_pairs={{0,32},{32,64},{64,96},{96,128},{128,160},{160,192},{192,224},{224... | collective-permute-start | bytes 49160 | tf_op jit(solution)/shard_map/ppermute | solution.py:26
  11.5 4.9 %collective-permute-start.3 = (f32[4,6,1,32]{3,2,1,0:T(1,128)S(1)}, f32[4,6,1,32]{3,2,1,0:T(1,128)S(1)}, u32[]{:S(2)}, u32[]{:S(2)}) collective-permute-start(f32[4,6,1,32]{3,2,1,0:T(1,128)S(1)} %get-tuple-element.23), channel_id=1, source_target_pairs={{0,1},{1,2},{2,3},{3,4},{4,5},{5,6},{6,7},{7,8},{8,9},{9,10},{10,1... | collective-permute-start | bytes 9224 | tf_op jit(solution)/shard_map/ppermute | solution.py:26
  14.6 4.4 %collective-permute-start.2 = (f32[4,6,1,32]{3,2,1,0:T(1,128)S(1)}, f32[4,6,1,32]{3,2,1,0:T(1,128)S(1)}, u32[]{:S(2)}, u32[]{:S(2)}) collective-permute-start(f32[4,6,1,32]{3,2,1,0:T(1,128)S(1)} %get-tuple-element.24), channel_id=1, source_target_pairs={{1,0},{2,1},{3,2},{4,3},{5,4},{6,5},{7,6},{8,7},{9,8},{10,9},{11,1... | collective-permute-start | bytes 9224 | tf_op jit(solution)/shard_map/ppermute | solution.py:27
  19.1 0.8 copy-start
  19.1 0.9 copy-start.1
  30.7 7.6 %collective-permute-start.4 = (f32[4,1,32,32]{3,2,1,0:T(8,128)S(1)}, f32[4,1,32,32]{3,2,1,0:T(8,128)S(1)}, u32[]{:S(2)}, u32[]{:S(2)}) collective-permute-start(f32[4,1,32,32]{3,2,1,0:T(8,128)S(1)} %get-tuple-element.79), channel_id=1, source_target_pairs={{0,32},{32,64},{64,96},{96,128},{128,160},{160,192},{192,224},{224... | collective-permute-start | bytes 49160 | tf_op jit(solution)/shard_map/ppermute | solution.py:26
  36.3 6.8 %collective-permute-start.5 = (f32[4,1,32,32]{3,2,1,0:T(8,128)S(1)}, f32[4,1,32,32]{3,2,1,0:T(8,128)S(1)}, u32[]{:S(2)}, u32[]{:S(2)}) collective-permute-start(f32[4,1,32,32]{3,2,1,0:T(8,128)S(1)} %get-tuple-element.80), channel_id=1, source_target_pairs={{32,0},{64,32},{96,64},{128,96},{160,128},{192,160},{224,192},{256... | collective-permute-start | bytes 49160 | tf_op jit(solution)/shard_map/ppermute | solution.py:27
  43.2 4.4 %collective-permute-start.7 = (f32[4,6,1,32]{3,2,1,0:T(1,128)S(1)}, f32[4,6,1,32]{3,2,1,0:T(1,128)S(1)}, u32[]{:S(2)}, u32[]{:S(2)}) collective-permute-start(f32[4,6,1,32]{3,2,1,0:T(1,128)S(1)} %get-tuple-element.21), channel_id=1, source_target_pairs={{0,1},{1,2},{2,3},{3,4},{4,5},{5,6},{6,7},{7,8},{8,9},{9,10},{10,1... | collective-permute-start | bytes 9224 | tf_op jit(solution)/shard_map/ppermute | solution.py:26
  46.3 4.4 %collective-permute-start.6 = (f32[4,6,1,32]{3,2,1,0:T(1,128)S(1)}, f32[4,6,1,32]{3,2,1,0:T(1,128)S(1)}, u32[]{:S(2)}, u32[]{:S(2)}) collective-permute-start(f32[4,6,1,32]{3,2,1,0:T(1,128)S(1)} %get-tuple-element.22), channel_id=1, source_target_pairs={{1,0},{2,1},{3,2},{4,3},{5,4},{6,5},{7,6},{8,7},{9,8},{10,9},{11,1... | collective-permute-start | bytes 9224 | tf_op jit(solution)/shard_map/ppermute | solution.py:27
  61.6 5.4 %collective-permute-start.8 = (f32[4,1,32,32]{3,2,1,0:T(8,128)S(1)}, f32[4,1,32,32]{3,2,1,0:T(8,128)S(1)}, u32[]{:S(2)}, u32[]{:S(2)}) collective-permute-start(f32[4,1,32,32]{3,2,1,0:T(8,128)S(1)} %get-tuple-element.77), channel_id=1, source_target_pairs={{0,32},{32,64},{64,96},{96,128},{128,160},{160,192},{192,224},{224... | collective-permute-start | bytes 49160 | tf_op jit(solution)/shard_map/ppermute | solution.py:26
  64.9 1.9 copy-start.5
  64.9 6.8 %collective-permute-start.9 = (f32[4,1,32,32]{3,2,1,0:T(8,128)S(1)}, f32[4,1,32,32]{3,2,1,0:T(8,128)S(1)}, u32[]{:S(2)}, u32[]{:S(2)}) collective-permute-start(f32[4,1,32,32]{3,2,1,0:T(8,128)S(1)} %get-tuple-element.78), channel_id=1, source_target_pairs={{32,0},{64,32},{96,64},{128,96},{160,128},{192,160},{224,192},{256... | collective-permute-start | bytes 49160 | tf_op jit(solution)/shard_map/ppermute | solution.py:27
  71.7 6.2 %collective-permute-start.11 = (f32[4,6,1,32]{3,2,1,0:T(1,128)S(1)}, f32[4,6,1,32]{3,2,1,0:T(1,128)S(1)}, u32[]{:S(2)}, u32[]{:S(2)}) collective-permute-start(f32[4,6,1,32]{3,2,1,0:T(1,128)S(1)} %get-tuple-element.19), channel_id=1, source_target_pairs={{0,1},{1,2},{2,3},{3,4},{4,5},{5,6},{6,7},{7,8},{8,9},{9,10},{10,1... | collective-permute-start | bytes 9224 | tf_op jit(solution)/shard_map/ppermute | solution.py:26
  76.1 4.7 %collective-permute-start.10 = (f32[4,6,1,32]{3,2,1,0:T(1,128)S(1)}, f32[4,6,1,32]{3,2,1,0:T(1,128)S(1)}, u32[]{:S(2)}, u32[]{:S(2)}) collective-permute-start(f32[4,6,1,32]{3,2,1,0:T(1,128)S(1)} %get-tuple-element.20), channel_id=1, source_target_pairs={{1,0},{2,1},{3,2},{4,3},{5,4},{6,5},{7,6},{8,7},{9,8},{10,9},{11,1... | collective-permute-start | bytes 9224 | tf_op jit(solution)/shard_map/ppermute | solution.py:27
  91.7 5.6 %collective-permute-start.12 = (f32[4,1,32,32]{3,2,1,0:T(8,128)S(1)}, f32[4,1,32,32]{3,2,1,0:T(8,128)S(1)}, u32[]{:S(2)}, u32[]{:S(2)}) collective-permute-start(f32[4,1,32,32]{3,2,1,0:T(8,128)S(1)} %get-tuple-element.75), channel_id=1, source_target_pairs={{0,32},{32,64},{64,96},{96,128},{128,160},{160,192},{192,224},{224... | collective-permute-start | bytes 49160 | tf_op jit(solution)/shard_map/ppermute | solution.py:26
  94.7 6.8 %collective-permute-start.13 = (f32[4,1,32,32]{3,2,1,0:T(8,128)S(1)}, f32[4,1,32,32]{3,2,1,0:T(8,128)S(1)}, u32[]{:S(2)}, u32[]{:S(2)}) collective-permute-start(f32[4,1,32,32]{3,2,1,0:T(8,128)S(1)} %get-tuple-element.76), channel_id=1, source_target_pairs={{32,0},{64,32},{96,64},{128,96},{160,128},{192,160},{224,192},{256... | collective-permute-start | bytes 49160 | tf_op jit(solution)/shard_map/ppermute | solution.py:27
  101.5 21.4 %collective-permute-start.15 = (f32[4,6,1,32]{3,2,1,0:T(1,128)S(1)}, f32[4,6,1,32]{3,2,1,0:T(1,128)S(1)}, u32[]{:S(2)}, u32[]{:S(2)}) collective-permute-start(f32[4,6,1,32]{3,2,1,0:T(1,128)S(1)} %get-tuple-element.17), channel_id=1, source_target_pairs={{0,1},{1,2},{2,3},{3,4},{4,5},{5,6},{6,7},{7,8},{8,9},{9,10},{10,1... | collective-permute-start | bytes 9224 | tf_op jit(solution)/shard_map/ppermute | solution.py:26
  105.3 17.7 %collective-permute-start.14 = (f32[4,6,1,32]{3,2,1,0:T(1,128)S(1)}, f32[4,6,1,32]{3,2,1,0:T(1,128)S(1)}, u32[]{:S(2)}, u32[]{:S(2)}) collective-permute-start(f32[4,6,1,32]{3,2,1,0:T(1,128)S(1)} %get-tuple-element.18), channel_id=1, source_target_pairs={{1,0},{2,1},{3,2},{4,3},{5,4},{6,5},{7,6},{8,7},{9,8},{10,9},{11,1... | collective-permute-start | bytes 9224 | tf_op jit(solution)/shard_map/ppermute | solution.py:27
  107.7 29.5 %all-to-all-start.1 = ((f32[32,1,2,4,128]{4,3,2,1,0:T(4,128)}), f32[32,1,2,4,128]{4,3,2,1,0:T(4,128)S(1)}, u32[]{:S(2)}, u32[]{:S(2)}) async-start(f32[32,1,2,4,128]{4,3,2,1,0:T(4,128)} %copy.118), calls=%async_computation.1 | async-start | bytes 262144 | tf_op jit(solution)/shard_map/all_to_all | solution.py:170
  137.1 20.4 %all-to-all-start = ((f32[32,1,4,4,128]{4,3,2,1,0:T(4,128)}), f32[32,1,4,4,128]{4,3,2,1,0:T(4,128)S(1)}, u32[]{:S(2)}, u32[]{:S(2)}) async-start(f32[32,1,4,4,128]{4,3,2,1,0:T(4,128)} %copy.113), calls=%async_computation | async-start | bytes 524288 | tf_op jit(solution)/shard_map/all_to_all | solution.py:169
where the time goes:
time: 205 us; the launch traced here: 204 us
  other arithmetic  86.6 us (42%)
  starting transfers between devices  69.8 us (34%)
  waiting for transfers between devices  33.5 us (16%)
  local copies, waits for them, and re-layouts  12 us (6%)
    add x32, other arithmetic, advance(): components[channel] + step_size * (reluctivity * laplacian + coupled)  85.1 us
    ppermute x8, starting transfers between devices, with_halo(): before = lax.ppermute(last, axis, up)  31.6 us
    ppermute x8, waiting for transfers between devices, with_halo(): after = lax.ppermute(leading, axis, down)  22.5 us
    all_to_all x1, starting transfers between devices, on_device(): lax.all_to_all(pack(material), 'seg', split_axis=0, concat_axis=0, tiled=...  15.3 us
    ppermute x8, starting transfers between devices, with_halo(): after = lax.ppermute(leading, axis, down)  13.5 us
    all_to_all x1, waiting for transfers between devices, on_device(): lax.all_to_all(pack(blocks), 'seg', split_axis=0, concat_axis=0, tiled=True)  10.9 us
    all_to_all x1, starting transfers between devices, on_device(): lax.all_to_all(pack(blocks), 'seg', split_axis=0, concat_axis=0, tiled=True)  9.4 us
  transfers between devices with their start and end apart: 18, of which 7 were waited for; matrix products, arithmetic and copies ran while one was open for 10% of the time, Pallas kernels for 0%

commit v1 on v0

v1 whole, which is shorter than its diff:
```python
import jax
import jax.numpy as jnp
from jax import lax
from jax.experimental import pallas as pl
from jax.experimental.pallas import tpu as pltpu
from jax.sharding import PartitionSpec as P

BXC = 4
BYC = 16
BZC = 8
BLY = 2
BLZ = 4
STEPS1 = 4
STEPS2 = 4
ROWS = BLY * BLZ
LANES = BYC * BZC
CH = 6
SLABS = CH * BXC
FC = SLABS * ROWS
HFC = FC + ROWS
LOW = HFC + ROWS
HIGH = LOW + SLABS
PACK = HIGH + SLABS
EXT = 3 * BXC
step_size = 0.05

VMEM = pl.BlockSpec(memory_space=pltpu.VMEM)
SMEM = pl.BlockSpec(memory_space=pltpu.SMEM)


def iotas():
    row = lax.broadcasted_iota(jnp.int32, (ROWS, LANES), 0)
    lane = lax.broadcasted_iota(jnp.int32, (ROWS, LANES), 1)
    return row, lane


def lanes_of(rows):
    return lax.broadcasted_iota(jnp.int32, (rows, LANES), 1)


def lroll(value, shift):
    return value if shift % LANES == 0 else pltpu.roll(value, shift % LANES, 1)


def sroll(value, shift):
    return pltpu.roll(value, shift % ROWS, 0)


def pack_kernel(field_ref, base_ref, rate_ref, contact_ref, own_ref, up_ref, down_ref, wide):
    cells = BLY * BYC
    parts = ((field_ref, 0, 4 * BXC), (base_ref, 4 * BXC, BXC), (rate_ref, 5 * BXC, BXC))
    wide[...] = jnp.zeros_like(wide)
    for ref, first, count in parts:
        wide[pl.ds(first * cells, count * cells), 0 : BLZ * BZC] = ref[...]
    count = SLABS * BLY
    group = lanes_of(count) // BZC
    placed = [None] * BLZ
    for yi in range(BYC):
        value = wide[pl.ds(yi, count, stride=BYC), :]
        for kz in range(BLZ):
            moved = lroll(value, BZC * (yi - kz))
            placed[kz] = moved if yi == 0 else jnp.where(group == yi, moved, placed[kz])
    for kz in range(BLZ):
        own_ref[pl.ds(kz, count, stride=BLZ), :] = placed[kz]
    contact = jnp.zeros((ROWS, LANES), jnp.float32)
    own_ref[pl.ds(FC, ROWS), :] = contact
    own_ref[pl.ds(FC, ROWS), 0:6] = contact_ref[...].astype(jnp.float32)
    quarter = lanes_of(SLABS) // (LANES // 4)
    for ref, jy, start in ((up_ref, BLY - 1, LANES - LANES // 4), (down_ref, 0, 0)):
        edge = None
        for kz in range(BLZ):
            value = own_ref[pl.ds(jy * BLZ + kz, SLABS, stride=ROWS), :]
            moved = lroll(value, kz * (LANES // 4) - start)
            edge = moved if kz == 0 else jnp.where(quarter == kz, moved, edge)
        ref[pl.ds(0, SLABS), :] = edge
        ref[pl.ds(SLABS, ROWS), :] = own_ref[pl.ds(FC, ROWS), :]


def join_kernel(own_ref, below_ref, above_ref, out_ref):
    row, _ = iotas()
    out_ref[pl.ds(0, HFC), :] = own_ref[...]
    below = sroll(below_ref[pl.ds(SLABS, ROWS), :], 4)
    above = sroll(above_ref[pl.ds(SLABS, ROWS), :], 4)
    out_ref[pl.ds(HFC, ROWS), :] = jnp.where(row < 4, below, above)
    out_ref[pl.ds(LOW, SLABS), :] = below_ref[pl.ds(0, SLABS), :]
    out_ref[pl.ds(HIGH, SLABS), :] = above_ref[pl.ds(0, SLABS), :]


def slot(i, channel):
    return (i // BXC) * SLABS + channel * BXC + i % BXC


def relax(differences, laplacian, values, base, rate, mix):
    e_xh, e_yh, e_zh = differences
    field_x = e_yh[2] - e_zh[1]
    field_y = e_zh[0] - e_xh[2]
    field_z = e_xh[1] - e_yh[0]
    saturation = rate * (field_x * field_x + field_y * field_y + field_z * field_z)
    reluctivity = base * (3.0 - 2.0 / (1.0 + saturation))
    updated = []
    for channel in range(4):
        total = reluctivity * laplacian[channel]
        for source in range(4):
            total = total + mix[channel][source] * values[source]
        updated.append(total)
    return updated


def update_kernel(
    mix_ref, owner_ref, own_ref, low_ref, high_ref, out_ref, inner, outer, cin, cout, done
):
    row, lane = iotas()
    kz, yi, zi = row % BLZ, lane // BZC, lane % BZC
    first_half = row < BLZ
    mix = [
        [step_size * mix_ref[c, e] + (1.0 if c == e else 0.0) for e in range(4)] for c in range(4)
    ]
    one = jnp.ones((ROWS, LANES), jnp.float32)

    for part, ref in enumerate((low_ref, own_ref, high_ref)):
        inner[0, pl.ds(part * FC, FC), :] = ref[pl.ds(0, FC), :]
        compact_low = ref[pl.ds(LOW, SLABS), :]
        compact_high = ref[pl.ds(HIGH, SLABS), :]
        wide_lane = lanes_of(SLABS)
        for k in range(BLZ):
            below = lroll(compact_low, LANES - (k + 1) * (LANES // 4))
            above = lroll(compact_high, -k * (LANES // 4))
            value = jnp.where(
                wide_lane < LANES // 4, above, jnp.where(wide_lane >= LANES - LANES // 4, below, 0.0)
            )
            outer[0, pl.ds(part * FC + k, SLABS, stride=ROWS), :] = value
            outer[0, pl.ds(part * FC + k + BLZ, SLABS, stride=ROWS), :] = value
        contact = ref[pl.ds(FC, ROWS), :]
        beside = ref[pl.ds(HFC, ROWS), :]
        turned = sroll(beside, BLZ)
        below = jnp.where(first_half, beside, turned)
        above = jnp.where(first_half, turned, beside)
        spread = lambda tile, d: jnp.broadcast_to(tile[:, d : d + 1], (ROWS, LANES))
        faces_in = [spread(contact, d) for d in range(6)]
        faces_out = [
            jnp.where(lane < LANES // 2, spread(above, d), spread(below, d)) for d in range(6)
        ]
        for coefficients, faces in ((cin, faces_in), (cout, faces_out)):
            ylow = jnp.where(yi == 0, faces[2], one)
            yhigh = jnp.where(yi == BYC - 1, faces[3], one)
            zlow = jnp.where(zi == 0, faces[4], one)
            zlow_n = jnp.where(jnp.logical_and(zi == 0, kz == 0), 0.0, zlow)
            zhigh = jnp.where(zi == BZC - 1, faces[5], one)
            zhigh_n = jnp.where(jnp.logical_and(zi == BZC - 1, kz == BLZ - 1), 0.0, zhigh)
            for x in range(BXC):
                xlow = faces[0] if x == 0 else one
                xhigh = faces[1] if x == BXC - 1 else one
                entries = (xlow, xhigh, ylow, yhigh, zlow_n, zhigh, zhigh_n, xlow + ylow + zlow)
                for d, entry in enumerate(entries):
                    coefficients[part * BXC + x, d] = entry

    def tile(ref, which, i, channel):
        at = pl.multiple_of(slot(i, channel) * ROWS, ROWS)
        return ref[which, pl.ds(at, ROWS), :]

    def sweep(now, i, with_outer):
        refs = (inner, outer) if with_outer else (inner,)
        coefs = (cin, cout)
        laps = [[], []]
        diffs = [([], [], []), ([], [], [])]
        values = [[], []]
        loaded = [
            [[cf[i, d] for d in range(8)] for cf in coefs[: len(refs)]],
        ][0]
        for c in range(4):
            u = tile(inner, now, i, c)
            h = tile(outer, now, i, c)
            u_up, h_up = lroll(u, -BZC), lroll(h, -BZC)
            u_down, h_down = lroll(u, BZC), lroll(h, BZC)
            turn_up, turn_down = sroll(u_up, BLZ), sroll(u_down, BLZ)
            here = [(u, u_up, u_down)] + ([(h, h_up, h_down)] if with_outer else [])
            over_up = [jnp.where(first_half, turn_up, h_up), jnp.where(first_half, u_up, turn_up)]
            over_down = [
                jnp.where(first_half, h_down, turn_down),
                jnp.where(first_half, turn_down, u_down),
            ]
            for part, (v, v_up, v_down) in enumerate(here):
                ref = refs[part]
                cxl, cxh, cyl, cyh, nzl, czh, nzh, low = loaded[part]
                n_yh = jnp.where(yi < BYC - 1, v_up, over_up[part])
                n_yl = jnp.where(yi > 0, v_down, over_down[part])
                n_zh = jnp.where(zi < BZC - 1, lroll(v, -1), sroll(lroll(v, BZC - 1), -1))
                n_zl = jnp.where(zi > 0, lroll(v, 1), sroll(lroll(v, 1 - BZC), 1))
                n_xl = tile(ref, now, i - 1, c)
                n_xh = tile(ref, now, i + 1, c)
                e_xh = cxh * (n_xh - v)
                e_yh = cyh * (n_yh - v)
                e_zh = nzh * n_zh - czh * v
                lap = cxl * n_xl + cyl * n_yl + nzl * n_zl - low * v
                laps[part].append(lap + (e_xh + e_yh + e_zh))
                diffs[part][0].append(e_xh)
                diffs[part][1].append(e_yh)
                diffs[part][2].append(e_zh)
                values[part].append(v)
        for part, ref in enumerate(refs):
            base = tile(ref, 0, i, 4) * step_size
            rate = tile(ref, 0, i, 5)
            updated = relax(diffs[part], laps[part], values[part], base, rate, mix)
            for c in range(4):
                at = pl.multiple_of(slot(i, c) * ROWS, ROWS)
                ref[1 - now, pl.ds(at, ROWS), :] = updated[c]

    for step in range(STEPS1):
        last = step == STEPS1 - 1

        def layer(i, carry, now=step % 2, with_outer=not last):
            sweep(now, i, with_outer)
            return carry

        lax.fori_loop(step + 1, EXT - 1 - step, layer, 0)

    y_inner = jnp.where(yi < BYC - 1, 1.0, 0.0)
    z_inner = jnp.where(zi < BZC - 1, 1.0, 0.0)
    y_low_inner = jnp.where(yi > 0, 1.0, 0.0)
    z_low_inner = jnp.where(zi > 0, 1.0, 0.0)
    out_ref[...] = jnp.zeros_like(out_ref)
    start = STEPS1 % 2
    state = [[tile(inner, start, BXC + x, c) for c in range(4)] for x in range(BXC)]
    for step in range(STEPS2):
        fresh = []
        rise = [
            [state[x + 1][c] - state[x][c] for c in range(4)] for x in range(BXC - 1)
        ]
        for x in range(BXC):
            laps, diffs = [], ([], [], [])
            for c in range(4):
                v = state[x][c]
                e_yh = y_inner * (lroll(v, -BZC) - v)
                e_zh = z_inner * (lroll(v, -1) - v)
                e_yl = y_low_inner * (lroll(v, BZC) - v)
                e_zl = z_low_inner * (lroll(v, 1) - v)
                lap = (e_yl + e_yh) + (e_zl + e_zh)
                if x < BXC - 1:
                    lap = lap + rise[x][c]
                if x > 0:
                    lap = lap - rise[x - 1][c]
                laps.append(lap)
                diffs[0].append(rise[x][c] if x < BXC - 1 else jnp.zeros_like(v))
                diffs[1].append(e_yh)
                diffs[2].append(e_zh)
            base = tile(inner, 0, BXC + x, 4) * step_size
            rate = tile(inner, 0, BXC + x, 5)
            fresh.append(relax(diffs, laps, state[x], base, rate, mix))
        state = fresh
    for x in range(BXC):
        for c in range(4):
            done[pl.ds((c * BXC + x) * ROWS, ROWS), :] = state[x][c]
    for block in range(ROWS):
        out_ref[owner_ref[0, block]] = done[pl.ds(block, 4 * BXC, stride=ROWS), :]


def on_device(initial_field, base_reluctivity, saturation_rate, mixing, face_contact, new_owner):
    f32 = jnp.float32
    cells = BLY * BYC
    peers = lax.axis_size("seg")
    own, up, down = pl.pallas_call(
        pack_kernel,
        out_shape=(
            jax.ShapeDtypeStruct((HFC, LANES), f32),
            jax.ShapeDtypeStruct((SLABS + ROWS, LANES), f32),
            jax.ShapeDtypeStruct((SLABS + ROWS, LANES), f32),
        ),
        in_specs=[VMEM] * 4,
        out_specs=(VMEM, VMEM, VMEM),
        scratch_shapes=[pltpu.VMEM((SLABS * cells, LANES), f32)],
        name="pack",
    )(
        initial_field.reshape(4 * BXC * cells, BLZ * BZC),
        base_reluctivity.reshape(BXC * cells, BLZ * BZC),
        saturation_rate.reshape(BXC * cells, BLZ * BZC),
        face_contact[0],
    )

    def both_ways(to_next, to_last, axis):
        size = lax.axis_size(axis)
        rising = [(i, i + 1) for i in range(size - 1)]
        falling = [(j, i) for i, j in rising]
        return lax.ppermute(to_next, axis, rising), lax.ppermute(to_last, axis, falling)

    below, above = both_ways(up, down, "seg")
    package = pl.pallas_call(
        join_kernel,
        out_shape=jax.ShapeDtypeStruct((PACK, LANES), f32),
        in_specs=[VMEM] * 3,
        out_specs=VMEM,
        name="join",
    )(own, below, above)
    low, high = both_ways(package, package, "grp")
    placed = pl.pallas_call(
        update_kernel,
        out_shape=jax.ShapeDtypeStruct((peers, 4 * BXC, LANES), f32),
        in_specs=[SMEM, SMEM, VMEM, VMEM, VMEM],
        out_specs=VMEM,
        scratch_shapes=[
            pltpu.VMEM((2, 3 * FC, LANES), f32),
            pltpu.VMEM((2, 3 * FC, LANES), f32),
            pltpu.VMEM((EXT, 8, ROWS, LANES), f32),
            pltpu.VMEM((EXT, 8, ROWS, LANES), f32),
            pltpu.VMEM((4 * BXC * ROWS, LANES), f32),
        ],
        name="update",
    )(mixing, new_owner, package, low, high)
    received = lax.all_to_all(placed, "seg", split_axis=0, concat_axis=0, tiled=True)
    return received.reshape(peers, 4, BXC, LANES)


def solution(mesh):
    return jax.shard_map(
        on_device,
        mesh=mesh,
        in_specs=(
            P(None, "grp", "seg", None),
            P("grp", "seg", None),
            P("grp", "seg", None),
            P(),
            P("grp", "seg", None),
            P("grp", "seg"),
        ),
        out_specs=P(("grp", "seg"), None, None, None),
        check_vma=False,
    )
```

time: 205 us -> 57.3 us (0.28)
  other arithmetic: 86.6 us -> 0 us
  starting transfers between devices: 69.8 us -> 13.5 us
  waiting for transfers between devices: 33.5 us -> 5.61 us
  blocking collectives: 0 us -> 24.6 us
  Pallas kernels: 0 us -> 9.88 us
  local copies, waits for them, and re-layouts: 12 us -> 3.31 us
    add x32 -> x0, other arithmetic: 85.1 us -> none  [advance(): components[channel] + step_size * (reluctivity * laplacian + coupled)]
    ppermute x16 -> x4, starting transfers between devices: 45.1 us -> 13.5 us  [the longest x2 8.21 us: both_ways(): lax.ppermute(to_next, axis, rising)]
    all_to_all x2 -> x0, starting transfers between devices: 24.7 us -> none  [the longest x1 15.3 us: on_device(): lax.all_to_all(pack(material), 'seg', split_axis=0, concat_axis=0, tiled=...]
    all_to_all x0 -> x1, blocking collectives: none -> 24.6 us  [on_device(): lax.all_to_all(placed, 'seg', split_axis=0, concat_axis=0, tiled=True)]
    ppermute x16 -> x4, waiting for transfers between devices: 22.6 us -> 5.61 us  [the longest x2 4.29 us: both_ways(): lax.ppermute(to_last, axis, falling)]
    all_to_all x2 -> x0, waiting for transfers between devices: 10.9 us -> none  [the longest x1 10.9 us: on_device(): lax.all_to_all(pack(blocks), 'seg', split_axis=0, concat_axis=0, tiled=True)]
    pallas_call x0 -> x3, Pallas kernels: none -> 9.88 us  [the longest x1 6.13 us: on_device(): pl.pallas_call(update_kernel, out_shape=jax.ShapeDtypeStruct((peers, 4 *...]
    slice x27 -> x0, local copies, waits for them, and re-layouts: 3.95 us -> none  [the longest x8 1.09 us: block_steps(): jnp.roll(state, -BZC, 3)]
  transfers between devices with their start and end apart: 18 -> 4, of which waited for: 7 -> 3; matrix products, arithmetic and copies ran while one was open for 10% -> 0% of each run, Pallas kernels for 0% -> 0%
where the time goes in v1:
time: 57.3 us; the launch traced here: 56.9 us
  blocking collectives  24.6 us (43%)
  starting transfers between devices  13.5 us (24%)
  Pallas kernels  9.88 us (17%)
  waiting for transfers between devices  5.61 us (10%)
  local copies, waits for them, and re-layouts  3.31 us (6%)
    all_to_all x1, blocking collectives, on_device(): lax.all_to_all(placed, 'seg', split_axis=0, concat_axis=0, tiled=True)  24.6 us
    ppermute x2, starting transfers between devices, both_ways(): lax.ppermute(to_next, axis, rising)  8.21 us
    pallas_call x1, Pallas kernels, on_device(): pl.pallas_call(update_kernel, out_shape=jax.ShapeDtypeStruct((peers, 4 *...  6.13 us
    ppermute x2, starting transfers between devices, both_ways(): lax.ppermute(to_last, axis, falling)  5.29 us
    ppermute x2, waiting for transfers between devices, both_ways(): lax.ppermute(to_last, axis, falling)  4.29 us
    unnamed x10, local copies, waits for them, and re-layouts  3.31 us
    pallas_call x1, Pallas kernels, on_device(): pl.pallas_call(pack_kernel, out_shape=(jax.ShapeDtypeStruct((HFC, LANES),...  2.17 us
    pallas_call x1, Pallas kernels, on_device(): pl.pallas_call(join_kernel, out_shape=jax.ShapeDtypeStruct((PACK, LANES),...  1.57 us
  transfers between devices with their start and end apart: 4, of which 3 were waited for; matrix products, arithmetic and copies ran while one was open for 0% of the time, Pallas kernels for 0%

profile of v1, /device:TPU:193, one launch (start us, length us, event | category | flops | bytes accessed | tf_op | source)
XLA Modules:
  0.0 56.9 jit_solution(12097882942157811430)
XLA Ops:
  0.0 1.3 %copy.7 = s32[1,8,6]{2,1,0:T(8,128)} copy(s32[1,8,6]{1,0,2:T(1,128)} %param.10) | data formatting | bytes 384 | tf_op args[4]
  1.3 2.2 %pack.1 = (f32[200,128]{1,0:T(8,128)}, f32[32,128]{1,0:T(8,128)}, f32[32,128]{1,0:T(8,128)}) custom-call(f32[512,32]{1,0:T(8,128)} %bitcast.6, f32[128,32]{1,0:T(8,128)} %bitcast.7, f32[128,32]{1,0:T(8,128)} %bitcast.8, s32[8,6]{1,0:T(8,128)} %bitcast.9), custom_call_target="tpu_custom_call" | custom-call | tf_op jit(solution)/shard_map/pack/pallas_call | solution.py:261
  3.5 3.1 %collective-permute-start = (f32[32,128]{1,0:T(8,128)}, f32[32,128]{1,0:T(8,128)S(1)}, u32[]{:S(2)}, u32[]{:S(2)}) collective-permute-start(f32[32,128]{1,0:T(8,128)} %get-tuple-element.9), channel_id=1, source_target_pairs={{0,1},{1,2},{2,3},{3,4},{4,5},{5,6},{6,7},{7,8},{8,9},{9,10},{10,1... | collective-permute-start | bytes 49160 | tf_op jit(solution)/shard_map/ppermute | solution.py:283
  6.6 1.3 %collective-permute-start.1 = (f32[32,128]{1,0:T(8,128)}, f32[32,128]{1,0:T(8,128)S(1)}, u32[]{:S(2)}, u32[]{:S(2)}) collective-permute-start(f32[32,128]{1,0:T(8,128)} %get-tuple-element.10), channel_id=1, source_target_pairs={{1,0},{2,1},{3,2},{4,3},{5,4},{6,5},{7,6},{8,7},{9,8},{10,9},{11,1... | collective-permute-start | bytes 49160 | tf_op jit(solution)/shard_map/ppermute | solution.py:283
  7.9 0.0 collective-permute-done.below_ref
  7.9 0.0 copy-start.2
  8.0 3.4 %collective-permute-done.1.above_ref = f32[32,128]{1,0:T(8,128)S(1)} collective-permute-done((f32[32,128]{1,0:T(8,128)}, f32[32,128]{1,0:T(8,128)S(1)}, u32[]{:S(2)}, u32[]{:S(2)}) %collective-permute-start.1) | collective-permute-done | bytes 16416 | tf_op jit(solution)/shard_map/ppermute | solution.py:283
  11.3 0.0 copy-start.3
  11.3 0.0 copy-done.2
  11.3 0.6 %copy-done.3 = f32[32,128]{1,0:T(8,128)} copy-done((f32[32,128]{1,0:T(8,128)}, f32[32,128]{1,0:T(8,128)S(1)}, u32[]{:S(2)}) %copy-start.3) | copy-done | bytes 16408
  11.9 1.6 %join.1.own_ref = f32[256,128]{1,0:T(8,128)} custom-call(f32[200,128]{1,0:T(8,128)} %get-tuple-element.8.own_ref, f32[32,128]{1,0:T(8,128)} %copy-done.2, f32[32,128]{1,0:T(8,128)} %copy-done.3), custom_call_target="tpu_custom_call" | custom-call | tf_op jit(solution)/shard_map/join/pallas_call | solution.py:286
  13.5 4.0 %collective-permute-start.3 = (f32[256,128]{1,0:T(8,128)}, f32[256,128]{1,0:T(8,128)S(1)}, u32[]{:S(2)}, u32[]{:S(2)}) collective-permute-start(f32[256,128]{1,0:T(8,128)} %join.1.own_ref), channel_id=1, source_target_pairs={{32,0},{64,32},{96,64},{128,96},{160,128},{192,160},{224,192},{256... | collective-permute-start | bytes 393224 | tf_op jit(solution)/shard_map/ppermute | solution.py:283
  17.5 5.1 %collective-permute-start.2 = (f32[256,128]{1,0:T(8,128)}, f32[256,128]{1,0:T(8,128)S(1)}, u32[]{:S(2)}, u32[]{:S(2)}) collective-permute-start(f32[256,128]{1,0:T(8,128)} %join.1.own_ref), channel_id=1, source_target_pairs={{0,32},{32,64},{64,96},{96,128},{128,160},{160,192},{192,224},{224... | collective-permute-start | bytes 393224 | tf_op jit(solution)/shard_map/ppermute | solution.py:283
  22.6 0.9 %collective-permute-done.3.high_ref = f32[256,128]{1,0:T(8,128)S(1)} collective-permute-done((f32[256,128]{1,0:T(8,128)}, f32[256,128]{1,0:T(8,128)S(1)}, u32[]{:S(2)}, u32[]{:S(2)}) %collective-permute-start.3) | collective-permute-done | bytes 131104 | tf_op jit(solution)/shard_map/ppermute | solution.py:283
  23.5 0.0 copy-start
  23.6 1.3 %collective-permute-done.2.low_ref = f32[256,128]{1,0:T(8,128)S(1)} collective-permute-done((f32[256,128]{1,0:T(8,128)}, f32[256,128]{1,0:T(8,128)S(1)}, u32[]{:S(2)}, u32[]{:S(2)}) %collective-permute-start.2) | collective-permute-done | bytes 131104 | tf_op jit(solution)/shard_map/ppermute | solution.py:283
  24.9 0.0 copy-done
  24.9 0.0 copy-start.1
  24.9 0.7 %copy-done.1 = f32[256,128]{1,0:T(8,128)} copy-done((f32[256,128]{1,0:T(8,128)}, f32[256,128]{1,0:T(8,128)S(1)}, u32[]{:S(2)}) %copy-start.1) | copy-done | bytes 131096
  25.5 6.1 %update.1 = f32[32,16,128]{2,1,0:T(8,128)} custom-call(f32[4,4]{1,0:T(4,128)} %mix_ref.1, s32[1,8]{1,0:T(1,128)} %owner_ref.1, f32[256,128]{1,0:T(8,128)} %join.1.own_ref, f32[256,128]{1,0:T(8,128)} %copy-done.1, f32[256,128]{1,0:T(8,128)} %copy-done), custom_call_target="tpu_custom_call" | custom-call | tf_op jit(solution)/shard_map/update/pallas_call | solution.py:294
  31.7 24.6 %all_to_all.5 = f32[32,16,128]{2,1,0:T(8,128)S(1)} all-to-all(f32[32,16,128]{2,1,0:T(8,128)} %update.1), channel_id=1, replica_groups=mesh['grp'=24,'seg'=32] {'seg'}, dimensions={0} | all-to-all | bytes 524288 | tf_op jit(solution)/shard_map/all_to_all | solution.py:308
  56.2 0.7 %copy.9 = f32[32,4,4,128]{3,2,1,0:T(4,128)} copy(f32[32,4,4,128]{3,2,1,0:T(4,128)S(1)} %bitcast.5) | data formatting | bytes 524288
Async XLA Ops:
  3.5 4.4 %collective-permute-start = (f32[32,128]{1,0:T(8,128)}, f32[32,128]{1,0:T(8,128)S(1)}, u32[]{:S(2)}, u32[]{:S(2)}) collective-permute-start(f32[32,128]{1,0:T(8,128)} %get-tuple-element.9), channel_id=1, source_target_pairs={{0,1},{1,2},{2,3},{3,4},{4,5},{5,6},{6,7},{7,8},{8,9},{9,10},{10,1... | collective-permute-start | bytes 49160 | tf_op jit(solution)/shard_map/ppermute | solution.py:283
  6.6 4.7 %collective-permute-start.1 = (f32[32,128]{1,0:T(8,128)}, f32[32,128]{1,0:T(8,128)S(1)}, u32[]{:S(2)}, u32[]{:S(2)}) collective-permute-start(f32[32,128]{1,0:T(8,128)} %get-tuple-element.10), channel_id=1, source_target_pairs={{1,0},{2,1},{3,2},{4,3},{5,4},{6,5},{7,6},{8,7},{9,8},{10,9},{11,1... | collective-permute-start | bytes 49160 | tf_op jit(solution)/shard_map/ppermute | solution.py:283
  7.9 3.4 %copy-start.2 = (f32[32,128]{1,0:T(8,128)}, f32[32,128]{1,0:T(8,128)S(1)}, u32[]{:S(2)}) copy-start(f32[32,128]{1,0:T(8,128)S(1)} %collective-permute-done.below_ref) | copy-start | bytes 49156
  11.3 0.6 %copy-start.3 = (f32[32,128]{1,0:T(8,128)}, f32[32,128]{1,0:T(8,128)S(1)}, u32[]{:S(2)}) copy-start(f32[32,128]{1,0:T(8,128)S(1)} %collective-permute-done.1.above_ref) | copy-start | bytes 49156
  13.5 10.0 %collective-permute-start.3 = (f32[256,128]{1,0:T(8,128)}, f32[256,128]{1,0:T(8,128)S(1)}, u32[]{:S(2)}, u32[]{:S(2)}) collective-permute-start(f32[256,128]{1,0:T(8,128)} %join.1.own_ref), channel_id=1, source_target_pairs={{32,0},{64,32},{96,64},{128,96},{160,128},{192,160},{224,192},{256... | collective-permute-start | bytes 393224 | tf_op jit(solution)/shard_map/ppermute | solution.py:283
  17.5 7.4 %collective-permute-start.2 = (f32[256,128]{1,0:T(8,128)}, f32[256,128]{1,0:T(8,128)S(1)}, u32[]{:S(2)}, u32[]{:S(2)}) collective-permute-start(f32[256,128]{1,0:T(8,128)} %join.1.own_ref), channel_id=1, source_target_pairs={{0,32},{32,64},{64,96},{96,128},{128,160},{160,192},{192,224},{224... | collective-permute-start | bytes 393224 | tf_op jit(solution)/shard_map/ppermute | solution.py:283
  23.5 1.3 %copy-start = (f32[256,128]{1,0:T(8,128)}, f32[256,128]{1,0:T(8,128)S(1)}, u32[]{:S(2)}) copy-start(f32[256,128]{1,0:T(8,128)S(1)} %collective-permute-done.3.high_ref) | copy-start | bytes 393220
  24.9 0.7 %copy-start.1 = (f32[256,128]{1,0:T(8,128)}, f32[256,128]{1,0:T(8,128)S(1)}, u32[]{:S(2)}) copy-start(f32[256,128]{1,0:T(8,128)S(1)} %collective-permute-done.2.low_ref) | copy-start | bytes 393220

commit v2 on v1

v2 whole, which is shorter than its diff:
```python
import jax
import jax.numpy as jnp
from jax import lax
from jax.experimental import pallas as pl
from jax.experimental.pallas import tpu as pltpu
from jax.sharding import PartitionSpec as P

BXC = 4
BYC = 16
BZC = 8
BLY = 2
BLZ = 4
STEPS1 = 4
STEPS2 = 4
ROWS = BLY * BLZ
LANES = BYC * BZC
CH = 6
SLABS = CH * BXC
FC = SLABS * ROWS
HFC = FC + ROWS
LOW = HFC + ROWS
HIGH = LOW + SLABS
PACK = HIGH + SLABS
EXT = 3 * BXC
step_size = 0.05

VMEM = pl.BlockSpec(memory_space=pltpu.VMEM)
SMEM = pl.BlockSpec(memory_space=pltpu.SMEM)


def iotas():
    row = lax.broadcasted_iota(jnp.int32, (ROWS, LANES), 0)
    lane = lax.broadcasted_iota(jnp.int32, (ROWS, LANES), 1)
    return row, lane


def lanes_of(rows):
    return lax.broadcasted_iota(jnp.int32, (rows, LANES), 1)


def lroll(value, shift):
    return value if shift % LANES == 0 else pltpu.roll(value, shift % LANES, 1)


def sroll(value, shift):
    return pltpu.roll(value, shift % ROWS, 0)


def pack_kernel(field_ref, base_ref, rate_ref, contact_ref, own_ref, up_ref, down_ref):
    first = 0
    for ref, slabs in ((field_ref, 4 * BXC), (base_ref, BXC), (rate_ref, BXC)):
        count = slabs * BLY
        group = lanes_of(count) // BZC % BLZ
        placed = [None] * BLZ
        for q in range(BLZ):
            mixed = jnp.concatenate(
                [ref[pl.ds(BLZ * r + q, count, stride=BYC), :] for r in range(BLZ)], axis=1
            )
            for kz in range(BLZ):
                moved = lroll(mixed, BZC * (q - kz))
                placed[kz] = moved if q == 0 else jnp.where(group == q, moved, placed[kz])
        for kz in range(BLZ):
            own_ref[pl.ds(first * ROWS + kz, count, stride=BLZ), :] = placed[kz]
        first += slabs
    row, lane = iotas()
    contact = jnp.zeros((ROWS, LANES), jnp.float32)
    for d in range(6):
        for block in range(ROWS):
            here = jnp.logical_and(row == block, lane == d)
            contact = jnp.where(here, contact_ref[d, block].astype(jnp.float32), contact)
    own_ref[pl.ds(FC, ROWS), :] = contact
    quarter = lanes_of(SLABS) // (LANES // 4)
    for ref, jy, start in ((up_ref, BLY - 1, LANES - LANES // 4), (down_ref, 0, 0)):
        edge = None
        for kz in range(BLZ):
            value = own_ref[pl.ds(jy * BLZ + kz, SLABS, stride=ROWS), :]
            moved = lroll(value, kz * (LANES // 4) - start)
            edge = moved if kz == 0 else jnp.where(quarter == kz, moved, edge)
        ref[pl.ds(0, SLABS), :] = edge
        ref[pl.ds(SLABS, ROWS), :] = contact


def join_kernel(own_ref, below_ref, above_ref, out_ref):
    row, _ = iotas()
    out_ref[pl.ds(0, HFC), :] = own_ref[...]
    below = sroll(below_ref[pl.ds(SLABS, ROWS), :], 4)
    above = sroll(above_ref[pl.ds(SLABS, ROWS), :], 4)
    out_ref[pl.ds(HFC, ROWS), :] = jnp.where(row < 4, below, above)
    out_ref[pl.ds(LOW, SLABS), :] = below_ref[pl.ds(0, SLABS), :]
    out_ref[pl.ds(HIGH, SLABS), :] = above_ref[pl.ds(0, SLABS), :]


def relax(differences, laplacian, values, base, rate, mix):
    e_xh, e_yh, e_zh = differences
    field_x = e_yh[2] - e_zh[1]
    field_y = e_zh[0] - e_xh[2]
    field_z = e_xh[1] - e_yh[0]
    saturation = rate * (field_x * field_x + field_y * field_y + field_z * field_z)
    reluctivity = base * (3.0 - 2.0 / (1.0 + saturation))
    updated = []
    for channel in range(4):
        total = reluctivity * laplacian[channel]
        for source in range(4):
            total = total + mix[channel][source] * values[source]
        updated.append(total)
    return updated


RING = 2 * ROWS
PAD = ROWS


def update_kernel(mix_ref, owner_ref, own_ref, low_ref, high_ref, out_ref, *scratch):
    ring, cin, done = scratch
    row, lane = iotas()
    kz, yi, zi = row % BLZ, lane // BZC, lane % BZC
    first_half = row < BLZ
    mix = [
        [step_size * mix_ref[c, e] + (1.0 if c == e else 0.0) for e in range(4)] for c in range(4)
    ]
    one = jnp.ones((ROWS, LANES), jnp.float32)
    zero = jnp.zeros((ROWS, LANES), jnp.float32)
    total = EXT * CH * RING

    def at(i, channel):
        return PAD + (i // BXC * SLABS + channel * BXC + i % BXC) * RING

    for now in range(2):
        ring[now, pl.ds(0, PAD), :] = zero
        ring[now, pl.ds(PAD + total, PAD), :] = zero
    for i, channel in ((0, 1), (0, 2), (0, 3), (0, 4), (BXC, 4)):
        ring[1, pl.ds(at(i, channel), ROWS), :] = zero
    for i, channel in ((BXC - 1, 5), (2 * BXC - 1, 5), (EXT - 1, 0), (EXT - 1, 1), (EXT - 1, 2)):
        ring[1, pl.ds(at(i, channel) + ROWS, ROWS), :] = zero
    faces = []
    for part, ref in enumerate((low_ref, own_ref, high_ref)):
        begin = PAD + part * SLABS * RING
        for slab in range(SLABS):
            ring[0, pl.ds(begin + slab * RING + BLZ, ROWS), :] = ref[pl.ds(slab * ROWS, ROWS), :]
        compact_low = ref[pl.ds(LOW, SLABS), :]
        compact_high = ref[pl.ds(HIGH, SLABS), :]
        wide_lane = lanes_of(SLABS)
        for k in range(BLZ):
            below = lroll(compact_low, LANES - (k + 1) * (LANES // 4))
            above = lroll(compact_high, -k * (LANES // 4))
            beyond = jnp.where(wide_lane >= LANES - LANES // 4, below, 0.0)
            beyond = jnp.where(wide_lane < LANES // 4, above, beyond)
            ring[0, pl.ds(begin + k, SLABS, stride=RING), :] = beyond
            ring[0, pl.ds(begin + k + 3 * BLZ, SLABS, stride=RING), :] = beyond
        contact = ref[pl.ds(FC, ROWS), :]
        beside = ref[pl.ds(HFC, ROWS), :]
        for d in range(6):
            ab = jnp.broadcast_to(contact[:, d : d + 1], (ROWS, LANES))
            ba = sroll(ab, BLZ)
            owners = jnp.broadcast_to(beside[:, d : d + 1], (ROWS, LANES))
            c = jnp.where(lane < LANES // 2, sroll(owners, BLZ), owners)
            ca = jnp.where(first_half, c, ba)
            bc = jnp.where(first_half, ba, sroll(c, BLZ))
            faces.append((ca, bc, ab))
    for part in range(3):
        for g in range(3):
            f = [faces[part * 6 + d][g] for d in range(6)]
            ylow = jnp.where(yi == 0, f[2], one)
            yhigh = jnp.where(yi == BYC - 1, f[3], one)
            zlow = jnp.where(zi == 0, f[4], one)
            zlow_n = jnp.where(jnp.logical_and(zi == 0, kz == 0), 0.0, zlow)
            zhigh = jnp.where(zi == BZC - 1, f[5], one)
            zhigh_n = jnp.where(jnp.logical_and(zi == BZC - 1, kz == BLZ - 1), 0.0, zhigh)
            entries = (ylow, yhigh, zlow_n, zhigh, zhigh_n, ylow + zlow, f[0], f[1])
            for d, entry in enumerate(entries):
                cin[part, g, d] = entry

    def put(now, start, value):
        ring[now, pl.ds(start, ROWS), :] = value

    def sweep(now, i, last):
        part, x = i // BXC, i % BXC
        groups = (2,) if last else (0, 1)
        offset = {0: 0, 1: ROWS, 2: BLZ}
        coefs = {g: [cin[part, g, d] for d in range(8)] for g in groups}
        laps = {g: [] for g in groups}
        diffs = {g: ([], [], []) for g in groups}
        values = {g: [] for g in groups}
        for c in range(4):
            start, before, after = at(i, c), at(i - 1, c), at(i + 1, c)

            def tile(begin):
                return ring[now, pl.ds(begin, ROWS), :]

            rows = [tile(start + offset[g]) for g in range(3)]
            following, previous = {0: 2, 1: 0, 2: 1}, {0: 1, 1: 2, 2: 0}
            ups = [lroll(v, -BZC) for v in rows]
            downs = [lroll(v, BZC) for v in rows]
            for g in groups:
                v = rows[g]
                cyl, cyh, nzl, czh, nzh, low, cxl, cxh = coefs[g]
                n_yh = jnp.where(yi < BYC - 1, ups[g], ups[following[g]])
                n_yl = jnp.where(yi > 0, downs[g], downs[previous[g]])
                z_next = lroll(tile(start + offset[g] + 1), BZC - 1)
                z_last = lroll(tile(start + offset[g] - 1), 1 - BZC)
                n_zh = jnp.where(zi < BZC - 1, lroll(v, -1), z_next)
                n_zl = jnp.where(zi > 0, lroll(v, 1), z_last)
                e_xl = v - tile(before + offset[g])
                if x == 0:
                    e_xl = cxl * e_xl
                e_xh = tile(after + offset[g]) - v
                if x == BXC - 1:
                    e_xh = cxh * e_xh
                e_yh = cyh * (n_yh - v)
                e_zh = nzh * n_zh - czh * v
                lap = (cyl * n_yl + nzl * n_zl) - low * v
                laps[g].append((lap - e_xl) + (e_xh + (e_yh + e_zh)))
                diffs[g][0].append(e_xh)
                diffs[g][1].append(e_yh)
                diffs[g][2].append(e_zh)
                values[g].append(v)
        for g in groups:
            base = ring[0, pl.ds(at(i, 4) + offset[g], ROWS), :] * step_size
            rate = ring[0, pl.ds(at(i, 5) + offset[g], ROWS), :]
            updated = relax(diffs[g], laps[g], values[g], base, rate, mix)
            if last:
                state[x] = updated
            else:
                for c in range(4):
                    put(1 - now, at(i, c) + offset[g], updated[c])

    state = [None] * BXC
    for step in range(STEPS1):
        for i in range(step + 1, EXT - 1 - step):
            sweep(step % 2, i, step == STEPS1 - 1)

    y_inner = jnp.where(yi < BYC - 1, 1.0, 0.0)
    z_inner = jnp.where(zi < BZC - 1, 1.0, 0.0)
    y_low_inner = jnp.where(yi > 0, 1.0, 0.0)
    z_low_inner = jnp.where(zi > 0, 1.0, 0.0)
    out_ref[...] = jnp.zeros_like(out_ref)
    for step in range(STEPS2):
        fresh = []
        rise = [[state[x + 1][c] - state[x][c] for c in range(4)] for x in range(BXC - 1)]
        rise.append([zero] * 4)
        for x in range(BXC):
            laps, diffs = [], ([], [], [])
            for c in range(4):
                v = state[x][c]
                e_yh = y_inner * (lroll(v, -BZC) - v)
                e_zh = z_inner * (lroll(v, -1) - v)
                e_yl = y_low_inner * (lroll(v, BZC) - v)
                e_zl = z_low_inner * (lroll(v, 1) - v)
                lap = (e_yl + e_yh) + (e_zl + e_zh)
                if x < BXC - 1:
                    lap = lap + rise[x][c]
                if x > 0:
                    lap = lap - rise[x - 1][c]
                laps.append(lap)
                diffs[0].append(rise[x][c])
                diffs[1].append(e_yh)
                diffs[2].append(e_zh)
            base = ring[0, pl.ds(at(BXC + x, 4) + BLZ, ROWS), :] * step_size
            rate = ring[0, pl.ds(at(BXC + x, 5) + BLZ, ROWS), :]
            fresh.append(relax(diffs, laps, state[x], base, rate, mix))
        state = fresh
    for x in range(BXC):
        for c in range(4):
            done[pl.ds((c * BXC + x) * ROWS, ROWS), :] = state[x][c]
    for block in range(ROWS):
        out_ref[owner_ref[0, block]] = done[pl.ds(block, 4 * BXC, stride=ROWS), :]


def on_device(initial_field, base_reluctivity, saturation_rate, mixing, face_contact, new_owner):
    f32 = jnp.float32
    cells = BLY * BYC
    peers = lax.axis_size("seg")
    own, up, down = pl.pallas_call(
        pack_kernel,
        out_shape=(
            jax.ShapeDtypeStruct((HFC, LANES), f32),
            jax.ShapeDtypeStruct((SLABS + ROWS, LANES), f32),
            jax.ShapeDtypeStruct((SLABS + ROWS, LANES), f32),
        ),
        in_specs=[VMEM, VMEM, VMEM, SMEM],
        out_specs=(VMEM, VMEM, VMEM),
        compiler_params=pltpu.CompilerParams(vmem_limit_bytes=4 << 20),
        name="pack",
    )(
        initial_field.reshape(4 * BXC * cells, BLZ * BZC),
        base_reluctivity.reshape(BXC * cells, BLZ * BZC),
        saturation_rate.reshape(BXC * cells, BLZ * BZC),
        face_contact[0].T,
    )

    def both_ways(to_next, to_last, axis):
        size = lax.axis_size(axis)
        rising = [(i, i + 1) for i in range(size - 1)]
        falling = [(j, i) for i, j in rising]
        return lax.ppermute(to_next, axis, rising), lax.ppermute(to_last, axis, falling)

    below, above = both_ways(up, down, "seg")
    package = pl.pallas_call(
        join_kernel,
        out_shape=jax.ShapeDtypeStruct((PACK, LANES), f32),
        in_specs=[VMEM] * 3,
        out_specs=VMEM,
        compiler_params=pltpu.CompilerParams(vmem_limit_bytes=4 << 20),
        name="join",
    )(own, below, above)
    low, high = both_ways(package, package, "grp")
    placed = pl.pallas_call(
        update_kernel,
        out_shape=jax.ShapeDtypeStruct((peers, 4 * BXC, LANES), f32),
        in_specs=[SMEM, SMEM, VMEM, VMEM, VMEM],
        out_specs=VMEM,
        scratch_shapes=[
            pltpu.VMEM((2, EXT * CH * RING + 2 * PAD, LANES), f32),
            pltpu.VMEM((3, 3, 8, ROWS, LANES), f32),
            pltpu.VMEM((4 * BXC * ROWS, LANES), f32),
        ],
        compiler_params=pltpu.CompilerParams(vmem_limit_bytes=8 << 20),
        name="update",
    )(mixing, new_owner, package, low, high)
    received = lax.all_to_all(placed, "seg", split_axis=0, concat_axis=0, tiled=True)
    return received.reshape(peers, 4, BXC, LANES)


def solution(mesh):
    return jax.shard_map(
        on_device,
        mesh=mesh,
        in_specs=(
            P(None, "grp", "seg", None),
            P("grp", "seg", None),
            P("grp", "seg", None),
            P(),
            P("grp", "seg", None),
            P("grp", "seg"),
        ),
        out_specs=P(("grp", "seg"), None, None, None),
        check_vma=False,
    )
```

time: 57.3 us -> 51.5 us (0.90)
  Pallas kernels: 9.88 us -> 3.77 us
  local copies, waits for them, and re-layouts: 3.31 us -> 4.02 us
    pallas_call x1, Pallas kernels: 6.13 us -> 2.78 us  [on_device(): pl.pallas_call(update_kernel, out_shape=jax.ShapeDtypeStruct((peers, 4 *...]
    pallas_call x1, Pallas kernels: 1.57 us -> 0.01 us  [on_device(): pl.pallas_call(join_kernel, out_shape=jax.ShapeDtypeStruct((PACK, LANES),...]
    pallas_call x1, Pallas kernels: 2.17 us -> 0.98 us  [on_device(): pl.pallas_call(pack_kernel, out_shape=(jax.ShapeDtypeStruct((HFC, LANES),...]
    squeeze x0 -> x1, local copies, waits for them, and re-layouts: none -> 0.68 us  [on_device(): face_contact[0]]
    unnamed x10 -> x11, local copies, waits for them, and re-layouts: 3.31 us -> 3.34 us
where the time goes in v2:
time: 51.5 us; the launch traced here: 51.1 us
  blocking collectives  24.5 us (48%)
  starting transfers between devices  13.7 us (27%)
  waiting for transfers between devices  5.1 us (10%)
  local copies, waits for them, and re-layouts  4.02 us (8%)
  Pallas kernels  3.77 us (7%)
    all_to_all x1, blocking collectives, on_device(): lax.all_to_all(placed, 'seg', split_axis=0, concat_axis=0, tiled=True)  24.5 us
    ppermute x2, starting transfers between devices, both_ways(): lax.ppermute(to_next, axis, rising)  8.22 us
    ppermute x2, starting transfers between devices, both_ways(): lax.ppermute(to_last, axis, falling)  5.44 us
    ppermute x2, waiting for transfers between devices, both_ways(): lax.ppermute(to_last, axis, falling)  3.88 us
    unnamed x11, local copies, waits for them, and re-layouts  3.34 us
    pallas_call x1, Pallas kernels, on_device(): pl.pallas_call(update_kernel, out_shape=jax.ShapeDtypeStruct((peers, 4 *...  2.78 us
    ppermute x2, waiting for transfers between devices, both_ways(): lax.ppermute(to_next, axis, rising)  1.22 us
  transfers between devices with their start and end apart: 4, of which 3 were waited for; matrix products, arithmetic and copies ran while one was open for 0% of the time, Pallas kernels for 0%

profile of v2, /device:TPU:193, one launch (start us, length us, event | category | flops | bytes accessed | tf_op | source)
XLA Modules:
  0.0 51.1 jit_solution(6442032162542414719)
XLA Ops:
  0.0 0.7 %copy.11 = s32[1,8,6]{1,2,0:T(8,128)S(1)} copy(s32[1,8,6]{1,0,2:T(1,128)} %param.10) | data formatting | bytes 384 | tf_op jit(solution)/shard_map/squeeze | solution.py:288
  0.7 0.0 copy-start
  0.7 0.9 %copy-done = f32[4,4,32,32]{3,2,1,0:T(8,128)S(1)} copy-done((f32[4,4,32,32]{3,2,1,0:T(8,128)S(1)}, f32[4,4,32,32]{3,2,1,0:T(8,128)}, u32[]{:S(2)}) %copy-start) | copy-done | bytes 65560
  1.6 0.0 copy-start.1
  1.6 0.8 %copy-done.1 = f32[4,32,32]{2,1,0:T(8,128)S(1)} copy-done((f32[4,32,32]{2,1,0:T(8,128)S(1)}, f32[4,32,32]{2,1,0:T(8,128)}, u32[]{:S(2)}) %copy-start.1) | copy-done | bytes 16408
  2.5 0.0 copy-start.2
  2.5 0.8 %copy-done.2 = f32[4,32,32]{2,1,0:T(8,128)S(1)} copy-done((f32[4,32,32]{2,1,0:T(8,128)S(1)}, f32[4,32,32]{2,1,0:T(8,128)}, u32[]{:S(2)}) %copy-start.2) | copy-done | bytes 16408
  3.3 1.0 %pack.1 = (f32[200,128]{1,0:T(8,128)S(1)}, f32[32,128]{1,0:T(8,128)S(1)}, f32[32,128]{1,0:T(8,128)S(1)}) custom-call(f32[512,32]{1,0:T(8,128)S(1)} %bitcast.10, f32[128,32]{1,0:T(8,128)S(1)} %bitcast.11, f32[128,32]{1,0:T(8,128)S(1)} %bitcast.12, s32[6,8]{1,0:T(8,128)S(1)} %bitcast.13), custom_call_target="tpu_custom_call" | custom-call | tf_op jit(solution)/shard_map/pack/pallas_call | solution.py:273
  4.3 3.1 %collective-permute-start = (f32[32,128]{1,0:T(8,128)S(1)}, f32[32,128]{1,0:T(8,128)S(1)}, u32[]{:S(2)}, u32[]{:S(2)}) collective-permute-start(f32[32,128]{1,0:T(8,128)S(1)} %get-tuple-element.9), channel_id=1, source_target_pairs={{0,1},{1,2},{2,3},{3,4},{4,5},{5,6},{6,7},{7,8},{8,9},{9,10},{10,1... | collective-permute-start | bytes 49160 | tf_op jit(solution)/shard_map/ppermute | solution.py:295
  7.4 1.3 %collective-permute-start.1 = (f32[32,128]{1,0:T(8,128)S(1)}, f32[32,128]{1,0:T(8,128)S(1)}, u32[]{:S(2)}, u32[]{:S(2)}) collective-permute-start(f32[32,128]{1,0:T(8,128)S(1)} %get-tuple-element.10), channel_id=1, source_target_pairs={{1,0},{2,1},{3,2},{4,3},{5,4},{6,5},{7,6},{8,7},{9,8},{10,9},{11,1... | collective-permute-start | bytes 49160 | tf_op jit(solution)/shard_map/ppermute | solution.py:295
  8.7 0.0 collective-permute-done.below_ref
  8.7 3.2 %collective-permute-done.1.above_ref = f32[32,128]{1,0:T(8,128)S(1)} collective-permute-done((f32[32,128]{1,0:T(8,128)S(1)}, f32[32,128]{1,0:T(8,128)S(1)}, u32[]{:S(2)}, u32[]{:S(2)}) %collective-permute-start.1) | collective-permute-done | bytes 16416 | tf_op jit(solution)/shard_map/ppermute | solution.py:295
  11.9 0.0 copy-start.3
  11.9 0.0 copy-start.4
  11.9 4.1 %collective-permute-start.3 = (f32[256,128]{1,0:T(8,128)S(1)}, f32[256,128]{1,0:T(8,128)S(1)}, u32[]{:S(2)}, u32[]{:S(2)}) collective-permute-start(f32[256,128]{1,0:T(8,128)S(1)} %join.1.own_ref), channel_id=1, source_target_pairs={{32,0},{64,32},{96,64},{128,96},{160,128},{192,160},{224,192},{256... | collective-permute-start | bytes 393224 | tf_op jit(solution)/shard_map/ppermute | solution.py:295
  16.1 5.1 %collective-permute-start.2 = (f32[256,128]{1,0:T(8,128)S(1)}, f32[256,128]{1,0:T(8,128)S(1)}, u32[]{:S(2)}, u32[]{:S(2)}) collective-permute-start(f32[256,128]{1,0:T(8,128)S(1)} %join.1.own_ref), channel_id=1, source_target_pairs={{0,32},{32,64},{64,96},{96,128},{128,160},{160,192},{192,224},{224... | collective-permute-start | bytes 393224 | tf_op jit(solution)/shard_map/ppermute | solution.py:295
  21.2 0.7 %collective-permute-done.3.high_ref = f32[256,128]{1,0:T(8,128)S(1)} collective-permute-done((f32[256,128]{1,0:T(8,128)S(1)}, f32[256,128]{1,0:T(8,128)S(1)}, u32[]{:S(2)}, u32[]{:S(2)}) %collective-permute-start.3) | collective-permute-done | bytes 131104 | tf_op jit(solution)/shard_map/ppermute | solution.py:295
  21.9 1.2 %collective-permute-done.2.low_ref = f32[256,128]{1,0:T(8,128)S(1)} collective-permute-done((f32[256,128]{1,0:T(8,128)S(1)}, f32[256,128]{1,0:T(8,128)S(1)}, u32[]{:S(2)}, u32[]{:S(2)}) %collective-permute-start.2) | collective-permute-done | bytes 131104 | tf_op jit(solution)/shard_map/ppermute | solution.py:295
  23.1 0.0 copy-done.3
  23.1 0.0 copy-done.4
  23.1 2.8 %update.1 = f32[32,16,128]{2,1,0:T(8,128)S(1)} custom-call(f32[4,4]{1,0:T(4,128)S(1)} %copy-done.3, s32[1,8]{1,0:T(1,128)S(1)} %copy-done.4, f32[256,128]{1,0:T(8,128)S(1)} %join.1.own_ref, f32[256,128]{1,0:T(8,128)S(1)} %collective-permute-done.2.low_ref, f32[256,128]{1,0:T(8,128)S(1)} %collective-permute-done.3.high_ref), custom_call_target="tpu_custom_call" | custom-call | tf_op jit(solution)/shard_map/update/pallas_call | solution.py:307
  25.9 24.5 %all_to_all.5 = f32[32,16,128]{2,1,0:T(8,128)S(1)} all-to-all(f32[32,16,128]{2,1,0:T(8,128)S(1)} %update.1), channel_id=1, replica_groups=mesh['grp'=24,'seg'=32] {'seg'}, dimensions={0} | all-to-all | bytes 524288 | tf_op jit(solution)/shard_map/all_to_all | solution.py:320
  50.4 0.7 %copy.13 = f32[32,4,4,128]{3,2,1,0:T(4,128)} copy(f32[32,4,4,128]{3,2,1,0:T(4,128)S(1)} %bitcast.14) | data formatting | bytes 524288
  (1 shorter events, 0.0 us)
Async XLA Ops:
  0.7 0.9 %copy-start = (f32[4,4,32,32]{3,2,1,0:T(8,128)S(1)}, f32[4,4,32,32]{3,2,1,0:T(8,128)}, u32[]{:S(2)}) copy-start(f32[4,4,32,32]{3,2,1,0:T(8,128)} %param.6) | copy-start | bytes 196612
  1.6 0.8 %copy-start.1 = (f32[4,32,32]{2,1,0:T(8,128)S(1)}, f32[4,32,32]{2,1,0:T(8,128)}, u32[]{:S(2)}) copy-start(f32[4,32,32]{2,1,0:T(8,128)} %param.7) | copy-start | bytes 49156
  2.5 0.8 %copy-start.2 = (f32[4,32,32]{2,1,0:T(8,128)S(1)}, f32[4,32,32]{2,1,0:T(8,128)}, u32[]{:S(2)}) copy-start(f32[4,32,32]{2,1,0:T(8,128)} %param.8) | copy-start | bytes 49156
  4.3 4.4 %collective-permute-start = (f32[32,128]{1,0:T(8,128)S(1)}, f32[32,128]{1,0:T(8,128)S(1)}, u32[]{:S(2)}, u32[]{:S(2)}) collective-permute-start(f32[32,128]{1,0:T(8,128)S(1)} %get-tuple-element.9), channel_id=1, source_target_pairs={{0,1},{1,2},{2,3},{3,4},{4,5},{5,6},{6,7},{7,8},{8,9},{9,10},{10,1... | collective-permute-start | bytes 49160 | tf_op jit(solution)/shard_map/ppermute | solution.py:295
  7.4 4.5 %collective-permute-start.1 = (f32[32,128]{1,0:T(8,128)S(1)}, f32[32,128]{1,0:T(8,128)S(1)}, u32[]{:S(2)}, u32[]{:S(2)}) collective-permute-start(f32[32,128]{1,0:T(8,128)S(1)} %get-tuple-element.10), channel_id=1, source_target_pairs={{1,0},{2,1},{3,2},{4,3},{5,4},{6,5},{7,6},{8,7},{9,8},{10,9},{11,1... | collective-permute-start | bytes 49160 | tf_op jit(solution)/shard_map/ppermute | solution.py:295
  11.9 11.2 %copy-start.3 = (f32[4,4]{1,0:T(4,128)S(1)}, f32[4,4]{1,0:T(4,128)}, u32[]{:S(2)}) copy-start(f32[4,4]{1,0:T(4,128)} %mix_ref.1) | copy-start | bytes 196
  11.9 11.2 %copy-start.4 = (s32[1,8]{1,0:T(1,128)S(1)}, s32[1,8]{1,0:T(1,128)}, u32[]{:S(2)}) copy-start(s32[1,8]{1,0:T(1,128)} %owner_ref.1) | copy-start | bytes 100
  11.9 10.0 %collective-permute-start.3 = (f32[256,128]{1,0:T(8,128)S(1)}, f32[256,128]{1,0:T(8,128)S(1)}, u32[]{:S(2)}, u32[]{:S(2)}) collective-permute-start(f32[256,128]{1,0:T(8,128)S(1)} %join.1.own_ref), channel_id=1, source_target_pairs={{32,0},{64,32},{96,64},{128,96},{160,128},{192,160},{224,192},{256... | collective-permute-start | bytes 393224 | tf_op jit(solution)/shard_map/ppermute | solution.py:295
  16.1 7.0 %collective-permute-start.2 = (f32[256,128]{1,0:T(8,128)S(1)}, f32[256,128]{1,0:T(8,128)S(1)}, u32[]{:S(2)}, u32[]{:S(2)}) collective-permute-start(f32[256,128]{1,0:T(8,128)S(1)} %join.1.own_ref), channel_id=1, source_target_pairs={{0,32},{32,64},{64,96},{96,128},{128,160},{160,192},{192,224},{224... | collective-permute-start | bytes 393224 | tf_op jit(solution)/shard_map/ppermute | solution.py:295

commit v3 on v2

--- a/solution.py
+++ b/solution.py
@@ -17,15 +17,14 @@
 CH = 6
 SLABS = CH * BXC
 FC = SLABS * ROWS
-HFC = FC + ROWS
-LOW = HFC + ROWS
-HIGH = LOW + SLABS
-PACK = HIGH + SLABS
+OWN = FC + ROWS
+EDGE = 3 * SLABS + 3 * ROWS
 EXT = 3 * BXC
 step_size = 0.05
 
 VMEM = pl.BlockSpec(memory_space=pltpu.VMEM)
 SMEM = pl.BlockSpec(memory_space=pltpu.SMEM)
+HBM = pl.BlockSpec(memory_space=pltpu.HBM)
 
 
 def iotas():
@@ -46,7 +45,26 @@
     return pltpu.roll(value, shift % ROWS, 0)
 
 
-def pack_kernel(field_ref, base_ref, rate_ref, contact_ref, own_ref, up_ref, down_ref):
+def pack_kernel(
+    field_hbm, base_hbm, rate_hbm, contact_ref, own_ref, field_ref, base_ref, rate_ref, sems
+):
+    copies = [
+        pltpu.make_async_copy(source, target, sems.at[n])
+        for n, (source, target) in enumerate(
+            ((field_hbm, field_ref), (base_hbm, base_ref), (rate_hbm, rate_ref))
+        )
+    ]
+    for copy in copies:
+        copy.start()
+    row, lane = iotas()
+    contact = jnp.zeros((ROWS, LANES), jnp.float32)
+    for d in range(6):
+        for block in range(ROWS):
+            here = jnp.logical_and(row == block, lane == d)
+            contact = jnp.where(here, contact_ref[d, 0, block].astype(jnp.float32), contact)
+    own_ref[pl.ds(FC, ROWS), :] = contact
+    for copy in copies:
+        copy.wait()
     first = 0
     for ref, slabs in ((field_ref, 4 * BXC), (base_ref, BXC), (rate_ref, BXC)):
         count = slabs * BLY
@@ -62,32 +80,30 @@
         for kz in range(BLZ):
             own_ref[pl.ds(first * ROWS + kz, count, stride=BLZ), :] = placed[kz]
         first += slabs
-    row, lane = iotas()
-    contact = jnp.zeros((ROWS, LANES), jnp.float32)
-    for d in range(6):
-        for block in range(ROWS):
-            here = jnp.logical_and(row == block, lane == d)
-            contact = jnp.where(here, contact_ref[d, block].astype(jnp.float32), contact)
-    own_ref[pl.ds(FC, ROWS), :] = contact
+
+
+def stage_kernel(own_ref, local_ref):
+    local_ref[...] = own_ref[...]
+
+
+def edge_kernel(own_ref, inside_ref, across_ref, second_ref, first_ref):
+    even = lax.axis_index("seg") % 2 == 0
     quarter = lanes_of(SLABS) // (LANES // 4)
-    for ref, jy, start in ((up_ref, BLY - 1, LANES - LANES // 4), (down_ref, 0, 0)):
-        edge = None
-        for kz in range(BLZ):
-            value = own_ref[pl.ds(jy * BLZ + kz, SLABS, stride=ROWS), :]
-            moved = lroll(value, kz * (LANES // 4) - start)
-            edge = moved if kz == 0 else jnp.where(quarter == kz, moved, edge)
-        ref[pl.ds(0, SLABS), :] = edge
-        ref[pl.ds(SLABS, ROWS), :] = contact
-
-
-def join_kernel(own_ref, below_ref, above_ref, out_ref):
-    row, _ = iotas()
-    out_ref[pl.ds(0, HFC), :] = own_ref[...]
-    below = sroll(below_ref[pl.ds(SLABS, ROWS), :], 4)
-    above = sroll(above_ref[pl.ds(SLABS, ROWS), :], 4)
-    out_ref[pl.ds(HFC, ROWS), :] = jnp.where(row < 4, below, above)
-    out_ref[pl.ds(LOW, SLABS), :] = below_ref[pl.ds(0, SLABS), :]
-    out_ref[pl.ds(HIGH, SLABS), :] = above_ref[pl.ds(0, SLABS), :]
+    for part, ref in enumerate((own_ref, inside_ref, across_ref)):
+        edges = []
+        for jy, start in ((BLY - 1, LANES - LANES // 4), (0, 0)):
+            edge = None
+            for kz in range(BLZ):
+                value = ref[pl.ds(jy * BLZ + kz, SLABS, stride=ROWS), :]
+                moved = lroll(value, kz * (LANES // 4) - start)
+                edge = moved if kz == 0 else jnp.where(quarter == kz, moved, edge)
+            edges.append(edge)
+        up, down = edges
+        contact = ref[pl.ds(FC, ROWS), :]
+        first_ref[pl.ds(part * SLABS, SLABS), :] = jnp.where(even, up, down)
+        second_ref[pl.ds(part * SLABS, SLABS), :] = jnp.where(even, down, up)
+        for out_ref in (first_ref, second_ref):
+            out_ref[pl.ds(3 * SLABS + part * ROWS, ROWS), :] = contact
 
 
 def relax(differences, laplacian, values, base, rate, mix):
@@ -110,14 +126,20 @@
 PAD = ROWS
 
 
-def update_kernel(mix_ref, owner_ref, own_ref, low_ref, high_ref, out_ref, *scratch):
-    ring, cin, done = scratch
+def update_kernel(mix_hbm, owner_hbm, own_ref, inside_ref, across_ref, first_ref, second_ref, out_ref, *scratch):
+    ring, cin, done, mix_ref, owner_ref, sems = scratch
+    copies = [
+        pltpu.make_async_copy(mix_hbm, mix_ref, sems.at[0]),
+        pltpu.make_async_copy(owner_hbm, owner_ref, sems.at[1]),
+    ]
+    for copy in copies:
+        copy.start()
+    even_x = lax.axis_index("grp") % 2 == 0
+    even_y = lax.axis_index("seg") % 2 == 0
+    places = (1, jnp.where(even_x, 2, 0), jnp.where(even_x, 0, 2))
     row, lane = iotas()
     kz, yi, zi = row % BLZ, lane // BZC, lane % BZC
     first_half = row < BLZ
-    mix = [
-        [step_size * mix_ref[c, e] + (1.0 if c == e else 0.0) for e in range(4)] for c in range(4)
-    ]
     one = jnp.ones((ROWS, LANES), jnp.float32)
     zero = jnp.zeros((ROWS, LANES), jnp.float32)
     total = EXT * CH * RING
@@ -132,13 +154,17 @@
         ring[1, pl.ds(at(i, channel), ROWS), :] = zero
     for i, channel in ((BXC - 1, 5), (2 * BXC - 1, 5), (EXT - 1, 0), (EXT - 1, 1), (EXT - 1, 2)):
         ring[1, pl.ds(at(i, channel) + ROWS, ROWS), :] = zero
-    faces = []
-    for part, ref in enumerate((low_ref, own_ref, high_ref)):
+    for n, ref in enumerate((own_ref, inside_ref, across_ref)):
+        part = places[n]
         begin = PAD + part * SLABS * RING
+        if n > 0:
+            begin = pl.multiple_of(begin, ROWS)
         for slab in range(SLABS):
             ring[0, pl.ds(begin + slab * RING + BLZ, ROWS), :] = ref[pl.ds(slab * ROWS, ROWS), :]
-        compact_low = ref[pl.ds(LOW, SLABS), :]
-        compact_high = ref[pl.ds(HIGH, SLABS), :]
+        first = first_ref[pl.ds(n * SLABS, SLABS), :]
+        second = second_ref[pl.ds(n * SLABS, SLABS), :]
+        compact_low = jnp.where(even_y, second, first)
+        compact_high = jnp.where(even_y, first, second)
         wide_lane = lanes_of(SLABS)
         for k in range(BLZ):
             below = lroll(compact_low, LANES - (k + 1) * (LANES // 4))
@@ -148,7 +174,10 @@
             ring[0, pl.ds(begin + k, SLABS, stride=RING), :] = beyond
             ring[0, pl.ds(begin + k + 3 * BLZ, SLABS, stride=RING), :] = beyond
         contact = ref[pl.ds(FC, ROWS), :]
-        beside = ref[pl.ds(HFC, ROWS), :]
+        first = first_ref[pl.ds(3 * SLABS + n * ROWS, ROWS), :]
+        second = second_ref[pl.ds(3 * SLABS + n * ROWS, ROWS), :]
+        faces = []
+        beside = sroll(jnp.where(first_half == even_y, first, second), BLZ)
         for d in range(6):
             ab = jnp.broadcast_to(contact[:, d : d + 1], (ROWS, LANES))
             ba = sroll(ab, BLZ)
@@ -157,9 +186,8 @@
             ca = jnp.where(first_half, c, ba)
             bc = jnp.where(first_half, ba, sroll(c, BLZ))
             faces.append((ca, bc, ab))
-    for part in range(3):
         for g in range(3):
-            f = [faces[part * 6 + d][g] for d in range(6)]
+            f = [faces[d][g] for d in range(6)]
             ylow = jnp.where(yi == 0, f[2], one)
             yhigh = jnp.where(yi == BYC - 1, f[3], one)
             zlow = jnp.where(zi == 0, f[4], one)
@@ -224,6 +252,11 @@
                 for c in range(4):
                     put(1 - now, at(i, c) + offset[g], updated[c])
 
+    for copy in copies:
+        copy.wait()
+    mix = [
+        [step_size * mix_ref[c, e] + (1.0 if c == e else 0.0) for e in range(4)] for c in range(4)
+    ]
     state = [None] * BXC
     for step in range(STEPS1):
         for i in range(step + 1, EXT - 1 - step):
@@ -234,7 +267,7 @@
     y_low_inner = jnp.where(yi > 0, 1.0, 0.0)
     z_low_inner = jnp.where(zi > 0, 1.0, 0.0)
     out_ref[...] = jnp.zeros_like(out_ref)
-    for step in range(STEPS2):
+    for _ in range(STEPS2):
         fresh = []
         rise = [[state[x + 1][c] - state[x][c] for c in range(4)] for x in range(BXC - 1)]
         rise.append([zero] * 4)
@@ -270,55 +303,74 @@
     f32 = jnp.float32
     cells = BLY * BYC
     peers = lax.axis_size("seg")
-    own, up, down = pl.pallas_call(
+    small = pltpu.CompilerParams(vmem_limit_bytes=4 << 20)
+    own = pl.pallas_call(
         pack_kernel,
-        out_shape=(
-            jax.ShapeDtypeStruct((HFC, LANES), f32),
-            jax.ShapeDtypeStruct((SLABS + ROWS, LANES), f32),
-            jax.ShapeDtypeStruct((SLABS + ROWS, LANES), f32),
-        ),
-        in_specs=[VMEM, VMEM, VMEM, SMEM],
-        out_specs=(VMEM, VMEM, VMEM),
-        compiler_params=pltpu.CompilerParams(vmem_limit_bytes=4 << 20),
+        out_shape=jax.ShapeDtypeStruct((OWN, LANES), f32),
+        in_specs=[HBM, HBM, HBM, SMEM],
+        out_specs=VMEM,
+        scratch_shapes=[
+            pltpu.VMEM((4 * BXC * cells, BLZ * BZC), f32),
+            pltpu.VMEM((BXC * cells, BLZ * BZC), f32),
+            pltpu.VMEM((BXC * cells, BLZ * BZC), f32),
+            pltpu.SemaphoreType.DMA((3,)),
+        ],
+        compiler_params=pltpu.CompilerParams(vmem_limit_bytes=66_900_000),
         name="pack",
     )(
         initial_field.reshape(4 * BXC * cells, BLZ * BZC),
         base_reluctivity.reshape(BXC * cells, BLZ * BZC),
         saturation_rate.reshape(BXC * cells, BLZ * BZC),
-        face_contact[0].T,
+        face_contact.transpose(2, 0, 1),
     )
 
-    def both_ways(to_next, to_last, axis):
-        size = lax.axis_size(axis)
-        rising = [(i, i + 1) for i in range(size - 1)]
-        falling = [(j, i) for i, j in rising]
-        return lax.ppermute(to_next, axis, rising), lax.ppermute(to_last, axis, falling)
-
-    below, above = both_ways(up, down, "seg")
-    package = pl.pallas_call(
-        join_kernel,
-        out_shape=jax.ShapeDtypeStruct((PACK, LANES), f32),
+    def swap(value, axis, offset):
+        pairs = [(i, i + 1) for i in range(offset, lax.axis_size(axis) - 1, 2)]
+        return lax.ppermute(value, axis, pairs + [(j, i) for i, j in pairs])
+
+    inside = swap(own, "grp", 0)
+    across = swap(own, "grp", 1)
+    own = pl.pallas_call(
+        stage_kernel,
+        out_shape=jax.ShapeDtypeStruct((OWN, LANES), f32),
+        in_specs=[VMEM],
+        out_specs=VMEM,
+        compiler_params=small,
+        name="stage_own",
+    )(own)
+    second, first = pl.pallas_call(
+        edge_kernel,
+        out_shape=(
+            jax.ShapeDtypeStruct((EDGE, LANES), f32),
+            jax.ShapeDtypeStruct((EDGE, LANES), f32),
+        ),
         in_specs=[VMEM] * 3,
-        out_specs=VMEM,
-        compiler_params=pltpu.CompilerParams(vmem_limit_bytes=4 << 20),
-        name="join",
-    )(own, below, above)
-    low, high = both_ways(package, package, "grp")
+        out_specs=(VMEM, VMEM),
+        compiler_params=small,
+        name="edge",
+    )(own, inside, across)
+    first = swap(first, "seg", 0)
+    second = swap(second, "seg", 1)
     placed = pl.pallas_call(
         update_kernel,
         out_shape=jax.ShapeDtypeStruct((peers, 4 * BXC, LANES), f32),
-        in_specs=[SMEM, SMEM, VMEM, VMEM, VMEM],
+        in_specs=[HBM, HBM] + [VMEM] * 5,
         out_specs=VMEM,
         scratch_shapes=[
             pltpu.VMEM((2, EXT * CH * RING + 2 * PAD, LANES), f32),
             pltpu.VMEM((3, 3, 8, ROWS, LANES), f32),
             pltpu.VMEM((4 * BXC * ROWS, LANES), f32),
+            pltpu.SMEM((4, 4), f32),
+            pltpu.SMEM((1, BLY * BLZ), jnp.int32),
+            pltpu.SemaphoreType.DMA((2,)),
         ],
         compiler_params=pltpu.CompilerParams(vmem_limit_bytes=8 << 20),
         name="update",
-    )(mixing, new_owner, package, low, high)
-    received = lax.all_to_all(placed, "seg", split_axis=0, concat_axis=0, tiled=True)
-    return received.reshape(peers, 4, BXC, LANES)
+    )(mixing, new_owner, own, inside, across, first, second)
+    received = lax.all_to_all(
+        placed.reshape(peers, 4, BXC, LANES), "seg", split_axis=0, concat_axis=0, tiled=True
+    )
+    return received
 
 
 def solution(mesh):

time: 51.5 us -> 47.8 us (0.928)
  the two profiles are of different devices: /device:TPU:193 before, /device:TPU:192 now
where the time goes in v3:
time: 47.8 us; the launch traced here: 47.5 us
  blocking collectives  26.6 us (56%)
  starting transfers between devices  11.6 us (24%)
  Pallas kernels  5.48 us (11%)
  waiting for transfers between devices  2.13 us (4%)
  local copies, waits for them, and re-layouts  1.6 us (3%)
    all_to_all x1, blocking collectives, on_device(): lax.all_to_all(placed.reshape(peers, 4, BXC, LANES), 'seg', split_axis=0,...  26.6 us
    ppermute x4, starting transfers between devices, swap(): return lax.ppermute(value, axis, pairs + [(j, i) for i, j in pairs])  11.6 us
    pallas_call x1, Pallas kernels, on_device(): pl.pallas_call(update_kernel, out_shape=jax.ShapeDtypeStruct((peers, 4 *...  2.7 us
    pallas_call x1, Pallas kernels, on_device(): pl.pallas_call(pack_kernel, out_shape=jax.ShapeDtypeStruct((OWN, LANES),...  2.65 us
    ppermute x4, waiting for transfers between devices, swap(): return lax.ppermute(value, axis, pairs + [(j, i) for i, j in pairs])  2.13 us
    unnamed x7, local copies, waits for them, and re-layouts  1.6 us
  transfers between devices with their start and end apart: 4, of which 2 were waited for; matrix products, arithmetic and copies ran while one was open for 0% of the time, Pallas kernels for 0%

profile of v3, /device:TPU:192, one launch (start us, length us, event | category | flops | bytes accessed | tf_op | source)
XLA Modules:
  0.0 47.5 jit_solution(6950426047517268073)
XLA Ops:
  0.0 2.6 %pack.1.own_ref = f32[200,128]{1,0:T(8,128)} custom-call(f32[512,32]{1,0:T(8,128)} %bitcast.6, f32[128,32]{1,0:T(8,128)} %bitcast.7, f32[128,32]{1,0:T(8,128)} %bitcast.8, s32[6,1,8]{2,1,0:T(1,128)} %bitcast.9), custom_call_target="tpu_custom_call" | custom-call | tf_op jit(solution)/shard_map/pack/pallas_call | solution.py:307
  2.7 1.9 %collective-permute-start.1 = (f32[200,128]{1,0:T(8,128)}, f32[200,128]{1,0:T(8,128)S(1)}, u32[]{:S(2)}, u32[]{:S(2)}) collective-permute-start(f32[200,128]{1,0:T(8,128)} %pack.1.own_ref), channel_id=1, source_target_pairs={{32,64},{96,128},{160,192},{224,256},{288,320},{352,384},{416,448}... | collective-permute-start | bytes 307208 | tf_op jit(solution)/shard_map/ppermute | solution.py:329
  4.6 5.6 %collective-permute-start = (f32[200,128]{1,0:T(8,128)}, f32[200,128]{1,0:T(8,128)S(1)}, u32[]{:S(2)}, u32[]{:S(2)}) collective-permute-start(f32[200,128]{1,0:T(8,128)} %pack.1.own_ref), channel_id=1, source_target_pairs={{0,32},{64,96},{128,160},{192,224},{256,288},{320,352},{384,416},{... | collective-permute-start | bytes 307208 | tf_op jit(solution)/shard_map/ppermute | solution.py:329
  10.2 0.0 copy-start
  10.2 0.9 %copy-done = f32[200,128]{1,0:T(8,128)S(1)} copy-done((f32[200,128]{1,0:T(8,128)S(1)}, f32[200,128]{1,0:T(8,128)}, u32[]{:S(2)}) %copy-start) | copy-done | bytes 102424
  11.1 0.0 collective-permute-done.1.across_ref
  11.1 0.2 collective-permute-done.inside_ref
  11.3 0.1 edge.1
  11.5 0.0 copy-start.1
  11.5 0.0 copy-start.2
  11.5 3.4 %collective-permute-start.2 = (f32[96,128]{1,0:T(8,128)S(1)}, f32[96,128]{1,0:T(8,128)S(1)}, u32[]{:S(2)}, u32[]{:S(2)}) collective-permute-start(f32[96,128]{1,0:T(8,128)S(1)} %get-tuple-element.7), channel_id=1, source_target_pairs={{0,1},{2,3},{4,5},{6,7},{8,9},{10,11},{12,13},{14,15},{16,17},{18,... | collective-permute-start | bytes 147464 | tf_op jit(solution)/shard_map/ppermute | solution.py:329
  14.9 0.7 %collective-permute-start.3 = (f32[96,128]{1,0:T(8,128)S(1)}, f32[96,128]{1,0:T(8,128)S(1)}, u32[]{:S(2)}, u32[]{:S(2)}) collective-permute-start(f32[96,128]{1,0:T(8,128)S(1)} %get-tuple-element.8), channel_id=1, source_target_pairs={{1,2},{3,4},{5,6},{7,8},{9,10},{11,12},{13,14},{15,16},{17,18},{19... | collective-permute-start | bytes 147464 | tf_op jit(solution)/shard_map/ppermute | solution.py:329
  15.6 1.9 %collective-permute-done.2.first_ref = f32[96,128]{1,0:T(8,128)S(1)} collective-permute-done((f32[96,128]{1,0:T(8,128)S(1)}, f32[96,128]{1,0:T(8,128)S(1)}, u32[]{:S(2)}, u32[]{:S(2)}) %collective-permute-start.2) | collective-permute-done | bytes 49184 | tf_op jit(solution)/shard_map/ppermute | solution.py:329
  17.5 0.0 collective-permute-done.3.second_ref
  17.5 0.0 copy-done.1
  17.5 0.0 copy-done.2
  17.5 2.7 %update.1 = f32[32,16,128]{2,1,0:T(8,128)S(1)} custom-call(f32[4,4]{1,0:T(4,128)S(1)} %copy-done.1, s32[1,8]{1,0:T(1,128)S(1)} %copy-done.2, f32[200,128]{1,0:T(8,128)S(1)} %stage_own.1.own_ref, f32[200,128]{1,0:T(8,128)S(1)} %collective-permute-done.inside_ref, f32[200,128]{1,0:T(8,128)S(1)} %collective-permute-done.1.across_ref, ...), custom_call_target="tpu_custom_call" | custom-call | tf_op jit(solution)/shard_map/update/pallas_call | solution.py:354
  20.2 26.6 %all_to_all.5 = f32[32,4,4,128]{3,2,1,0:T(4,128)S(1)} all-to-all(f32[32,4,4,128]{3,2,1,0:T(4,128)S(1)} %bitcast.5), channel_id=1, replica_groups=mesh['grp'=24,'seg'=32] {'seg'}, dimensions={0} | all-to-all | bytes 524288 | tf_op jit(solution)/shard_map/all_to_all | solution.py:370
  46.8 0.7 %copy.8 = f32[32,4,4,128]{3,2,1,0:T(4,128)} copy(f32[32,4,4,128]{3,2,1,0:T(4,128)S(1)} %all_to_all.5) | data formatting | bytes 524288
  (1 shorter events, 0.0 us)
Async XLA Ops:
  2.7 8.4 %collective-permute-start.1 = (f32[200,128]{1,0:T(8,128)}, f32[200,128]{1,0:T(8,128)S(1)}, u32[]{:S(2)}, u32[]{:S(2)}) collective-permute-start(f32[200,128]{1,0:T(8,128)} %pack.1.own_ref), channel_id=1, source_target_pairs={{32,64},{96,128},{160,192},{224,256},{288,320},{352,384},{416,448}... | collective-permute-start | bytes 307208 | tf_op jit(solution)/shard_map/ppermute | solution.py:329
  4.6 6.7 %collective-permute-start = (f32[200,128]{1,0:T(8,128)}, f32[200,128]{1,0:T(8,128)S(1)}, u32[]{:S(2)}, u32[]{:S(2)}) collective-permute-start(f32[200,128]{1,0:T(8,128)} %pack.1.own_ref), channel_id=1, source_target_pairs={{0,32},{64,96},{128,160},{192,224},{256,288},{320,352},{384,416},{... | collective-permute-start | bytes 307208 | tf_op jit(solution)/shard_map/ppermute | solution.py:329
  10.2 0.9 %copy-start = (f32[200,128]{1,0:T(8,128)S(1)}, f32[200,128]{1,0:T(8,128)}, u32[]{:S(2)}) copy-start(f32[200,128]{1,0:T(8,128)} %pack.1.own_ref) | copy-start | bytes 307204
  11.5 6.0 %copy-start.1 = (f32[4,4]{1,0:T(4,128)S(1)}, f32[4,4]{1,0:T(4,128)}, u32[]{:S(2)}) copy-start(f32[4,4]{1,0:T(4,128)} %mix_hbm.1) | copy-start | bytes 196
  11.5 6.0 %copy-start.2 = (s32[1,8]{1,0:T(1,128)S(1)}, s32[1,8]{1,0:T(1,128)}, u32[]{:S(2)}) copy-start(s32[1,8]{1,0:T(1,128)} %owner_hbm.1) | copy-start | bytes 100
  11.5 6.0 %collective-permute-start.2 = (f32[96,128]{1,0:T(8,128)S(1)}, f32[96,128]{1,0:T(8,128)S(1)}, u32[]{:S(2)}, u32[]{:S(2)}) collective-permute-start(f32[96,128]{1,0:T(8,128)S(1)} %get-tuple-element.7), channel_id=1, source_target_pairs={{0,1},{2,3},{4,5},{6,7},{8,9},{10,11},{12,13},{14,15},{16,17},{18,... | collective-permute-start | bytes 147464 | tf_op jit(solution)/shard_map/ppermute | solution.py:329
  14.9 2.6 %collective-permute-start.3 = (f32[96,128]{1,0:T(8,128)S(1)}, f32[96,128]{1,0:T(8,128)S(1)}, u32[]{:S(2)}, u32[]{:S(2)}) collective-permute-start(f32[96,128]{1,0:T(8,128)S(1)} %get-tuple-element.8), channel_id=1, source_target_pairs={{1,2},{3,4},{5,6},{7,8},{9,10},{11,12},{13,14},{15,16},{17,18},{19... | collective-permute-start | bytes 147464 | tf_op jit(solution)/shard_map/ppermute | solution.py:329

commit v4 on v3

--- a/solution.py
+++ b/solution.py
@@ -27,6 +27,10 @@
 HBM = pl.BlockSpec(memory_space=pltpu.HBM)
 
 
+def in_hbm(value):
+    return pltpu.with_memory_space_constraint(value, pltpu.HBM)
+
+
 def iotas():
     row = lax.broadcasted_iota(jnp.int32, (ROWS, LANES), 0)
     lane = lax.broadcasted_iota(jnp.int32, (ROWS, LANES), 1)
@@ -46,16 +50,31 @@
 
 
 def pack_kernel(
-    field_hbm, base_hbm, rate_hbm, contact_ref, own_ref, field_ref, base_ref, rate_ref, sems
+    field_hbm,
+    base_hbm,
+    rate_hbm,
+    contact_hbm,
+    own_ref,
+    field_ref,
+    base_ref,
+    rate_ref,
+    contact_ref,
+    sems,
 ):
     copies = [
         pltpu.make_async_copy(source, target, sems.at[n])
         for n, (source, target) in enumerate(
-            ((field_hbm, field_ref), (base_hbm, base_ref), (rate_hbm, rate_ref))
+            (
+                (contact_hbm, contact_ref),
+                (base_hbm, base_ref),
+                (rate_hbm, rate_ref),
+                (field_hbm, field_ref),
+            )
         )
     ]
     for copy in copies:
         copy.start()
+    copies[0].wait()
     row, lane = iotas()
     contact = jnp.zeros((ROWS, LANES), jnp.float32)
     for d in range(6):
@@ -63,7 +82,7 @@
             here = jnp.logical_and(row == block, lane == d)
             contact = jnp.where(here, contact_ref[d, 0, block].astype(jnp.float32), contact)
     own_ref[pl.ds(FC, ROWS), :] = contact
-    for copy in copies:
+    for copy in copies[1:]:
         copy.wait()
     first = 0
     for ref, slabs in ((field_ref, 4 * BXC), (base_ref, BXC), (rate_ref, BXC)):
@@ -80,10 +99,6 @@
         for kz in range(BLZ):
             own_ref[pl.ds(first * ROWS + kz, count, stride=BLZ), :] = placed[kz]
         first += slabs
-
-
-def stage_kernel(own_ref, local_ref):
-    local_ref[...] = own_ref[...]
 
 
 def edge_kernel(own_ref, inside_ref, across_ref, second_ref, first_ref):
@@ -307,21 +322,22 @@
     own = pl.pallas_call(
         pack_kernel,
         out_shape=jax.ShapeDtypeStruct((OWN, LANES), f32),
-        in_specs=[HBM, HBM, HBM, SMEM],
+        in_specs=[HBM] * 4,
         out_specs=VMEM,
         scratch_shapes=[
             pltpu.VMEM((4 * BXC * cells, BLZ * BZC), f32),
             pltpu.VMEM((BXC * cells, BLZ * BZC), f32),
             pltpu.VMEM((BXC * cells, BLZ * BZC), f32),
-            pltpu.SemaphoreType.DMA((3,)),
+            pltpu.SMEM((6, 1, ROWS), jnp.int32),
+            pltpu.SemaphoreType.DMA((4,)),
         ],
-        compiler_params=pltpu.CompilerParams(vmem_limit_bytes=66_900_000),
+        compiler_params=small,
         name="pack",
     )(
-        initial_field.reshape(4 * BXC * cells, BLZ * BZC),
-        base_reluctivity.reshape(BXC * cells, BLZ * BZC),
-        saturation_rate.reshape(BXC * cells, BLZ * BZC),
-        face_contact.transpose(2, 0, 1),
+        in_hbm(initial_field.reshape(4 * BXC * cells, BLZ * BZC)),
+        in_hbm(base_reluctivity.reshape(BXC * cells, BLZ * BZC)),
+        in_hbm(saturation_rate.reshape(BXC * cells, BLZ * BZC)),
+        in_hbm(face_contact.transpose(2, 0, 1)),
     )
 
     def swap(value, axis, offset):
@@ -330,14 +346,6 @@
 
     inside = swap(own, "grp", 0)
     across = swap(own, "grp", 1)
-    own = pl.pallas_call(
-        stage_kernel,
-        out_shape=jax.ShapeDtypeStruct((OWN, LANES), f32),
-        in_specs=[VMEM],
-        out_specs=VMEM,
-        compiler_params=small,
-        name="stage_own",
-    )(own)
     second, first = pl.pallas_call(
         edge_kernel,
         out_shape=(
@@ -366,7 +374,7 @@
         ],
         compiler_params=pltpu.CompilerParams(vmem_limit_bytes=8 << 20),
         name="update",
-    )(mixing, new_owner, own, inside, across, first, second)
+    )(in_hbm(mixing), in_hbm(new_owner), own, inside, across, first, second)
     received = lax.all_to_all(
         placed.reshape(peers, 4, BXC, LANES), "seg", split_axis=0, concat_axis=0, tiled=True
     )

time: 47.8 us -> 46.6 us (0.975)
  Pallas kernels: 5.48 us -> 4.46 us
  local copies, waits for them, and re-layouts: 1.6 us -> 0.7 us
  waiting for transfers between devices: 2.13 us -> 2.83 us
    pallas_call x1, Pallas kernels: 2.65 us -> 1.39 us  [on_device(): pl.pallas_call(pack_kernel, out_shape=jax.ShapeDtypeStruct((OWN, LANES),...]
    unnamed x7 -> x1, local copies, waits for them, and re-layouts: 1.6 us -> 0.7 us
    ppermute x4, waiting for transfers between devices: 2.13 us -> 2.83 us  [swap(): return lax.ppermute(value, axis, pairs + [(j, i) for i, j in pairs])]
where the time goes in v4:
time: 46.6 us; the launch traced here: 46.3 us
  blocking collectives  26.6 us (57%)
  starting transfers between devices  11.6 us (25%)
  Pallas kernels  4.46 us (10%)
  waiting for transfers between devices  2.83 us (6%)
  local copies, waits for them, and re-layouts  0.7 us (2%)
    all_to_all x1, blocking collectives, on_device(): lax.all_to_all(placed.reshape(peers, 4, BXC, LANES), 'seg', split_axis=0,...  26.6 us
    ppermute x4, starting transfers between devices, swap(): return lax.ppermute(value, axis, pairs + [(j, i) for i, j in pairs])  11.6 us
    pallas_call x1, Pallas kernels, on_device(): pl.pallas_call(update_kernel, out_shape=jax.ShapeDtypeStruct((peers, 4 *...  2.95 us
    ppermute x4, waiting for transfers between devices, swap(): return lax.ppermute(value, axis, pairs + [(j, i) for i, j in pairs])  2.83 us
    pallas_call x1, Pallas kernels, on_device(): pl.pallas_call(pack_kernel, out_shape=jax.ShapeDtypeStruct((OWN, LANES),...  1.39 us
  transfers between devices with their start and end apart: 4, of which 2 were waited for; matrix products, arithmetic and copies ran while one was open for 0% of the time, Pallas kernels for 0%

profile of v4, /device:TPU:192, one launch (start us, length us, event | category | flops | bytes accessed | tf_op | source)
XLA Modules:
  0.0 46.3 jit_solution(244060883120065876)
XLA Ops:
  0.0 1.4 %pack.1.own_ref = f32[200,128]{1,0:T(8,128)S(1)} custom-call(f32[512,32]{1,0:T(8,128)} %bitcast.6, f32[128,32]{1,0:T(8,128)} %bitcast.7, f32[128,32]{1,0:T(8,128)} %bitcast.8, s32[6,1,8]{2,1,0:T(1,128)} %bitcast.9), custom_call_target="tpu_custom_call" | custom-call | tf_op jit(solution)/shard_map/pack/pallas_call | solution.py:322
  1.4 1.9 %collective-permute-start.1 = (f32[200,128]{1,0:T(8,128)S(1)}, f32[200,128]{1,0:T(8,128)S(1)}, u32[]{:S(2)}, u32[]{:S(2)}) collective-permute-start(f32[200,128]{1,0:T(8,128)S(1)} %pack.1.own_ref), channel_id=1, source_target_pairs={{32,64},{96,128},{160,192},{224,256},{288,320},{352,384},{416,448}... | collective-permute-start | bytes 307208 | tf_op jit(solution)/shard_map/ppermute | solution.py:345
  3.3 5.6 %collective-permute-start = (f32[200,128]{1,0:T(8,128)S(1)}, f32[200,128]{1,0:T(8,128)S(1)}, u32[]{:S(2)}, u32[]{:S(2)}) collective-permute-start(f32[200,128]{1,0:T(8,128)S(1)} %pack.1.own_ref), channel_id=1, source_target_pairs={{0,32},{64,96},{128,160},{192,224},{256,288},{320,352},{384,416},{... | collective-permute-start | bytes 307208 | tf_op jit(solution)/shard_map/ppermute | solution.py:345
  8.9 0.0 collective-permute-done.1.across_ref
  8.9 0.9 %collective-permute-done.inside_ref = f32[200,128]{1,0:T(8,128)S(1)} collective-permute-done((f32[200,128]{1,0:T(8,128)S(1)}, f32[200,128]{1,0:T(8,128)S(1)}, u32[]{:S(2)}, u32[]{:S(2)}) %collective-permute-start) | collective-permute-done | bytes 102432 | tf_op jit(solution)/shard_map/ppermute | solution.py:345
  9.9 0.1 edge.1
  10.0 3.4 %collective-permute-start.2 = (f32[96,128]{1,0:T(8,128)S(1)}, f32[96,128]{1,0:T(8,128)S(1)}, u32[]{:S(2)}, u32[]{:S(2)}) collective-permute-start(f32[96,128]{1,0:T(8,128)S(1)} %get-tuple-element.7), channel_id=1, source_target_pairs={{0,1},{2,3},{4,5},{6,7},{8,9},{10,11},{12,13},{14,15},{16,17},{18,... | collective-permute-start | bytes 147464 | tf_op jit(solution)/shard_map/ppermute | solution.py:345
  13.4 0.7 %collective-permute-start.3 = (f32[96,128]{1,0:T(8,128)S(1)}, f32[96,128]{1,0:T(8,128)S(1)}, u32[]{:S(2)}, u32[]{:S(2)}) collective-permute-start(f32[96,128]{1,0:T(8,128)S(1)} %get-tuple-element.8), channel_id=1, source_target_pairs={{1,2},{3,4},{5,6},{7,8},{9,10},{11,12},{13,14},{15,16},{17,18},{19... | collective-permute-start | bytes 147464 | tf_op jit(solution)/shard_map/ppermute | solution.py:345
  14.1 1.9 %collective-permute-done.2.first_ref = f32[96,128]{1,0:T(8,128)S(1)} collective-permute-done((f32[96,128]{1,0:T(8,128)S(1)}, f32[96,128]{1,0:T(8,128)S(1)}, u32[]{:S(2)}, u32[]{:S(2)}) %collective-permute-start.2) | collective-permute-done | bytes 49184 | tf_op jit(solution)/shard_map/ppermute | solution.py:345
  16.0 0.0 collective-permute-done.3.second_ref
  16.0 3.0 %update.1 = f32[32,16,128]{2,1,0:T(8,128)S(1)} custom-call(f32[4,4]{1,0:T(4,128)} %mix_hbm.1, s32[1,8]{1,0:T(1,128)} %owner_hbm.1, f32[200,128]{1,0:T(8,128)S(1)} %pack.1.own_ref, f32[200,128]{1,0:T(8,128)S(1)} %collective-permute-done.inside_ref, f32[200,128]{1,0:T(8,128)S(1)} %collective-permute-done.1.across_ref, ...), custom_call_target="tpu_custom_call" | custom-call | tf_op jit(solution)/shard_map/update/pallas_call | solution.py:362
  18.9 26.6 %all_to_all.5 = f32[32,4,4,128]{3,2,1,0:T(4,128)S(1)} all-to-all(f32[32,4,4,128]{3,2,1,0:T(4,128)S(1)} %bitcast.5), channel_id=1, replica_groups=mesh['grp'=24,'seg'=32] {'seg'}, dimensions={0} | all-to-all | bytes 524288 | tf_op jit(solution)/shard_map/all_to_all | solution.py:378
  45.6 0.7 %copy.8 = f32[32,4,4,128]{3,2,1,0:T(4,128)} copy(f32[32,4,4,128]{3,2,1,0:T(4,128)S(1)} %all_to_all.5) | data formatting | bytes 524288
Async XLA Ops:
  1.4 7.5 %collective-permute-start.1 = (f32[200,128]{1,0:T(8,128)S(1)}, f32[200,128]{1,0:T(8,128)S(1)}, u32[]{:S(2)}, u32[]{:S(2)}) collective-permute-start(f32[200,128]{1,0:T(8,128)S(1)} %pack.1.own_ref), channel_id=1, source_target_pairs={{32,64},{96,128},{160,192},{224,256},{288,320},{352,384},{416,448}... | collective-permute-start | bytes 307208 | tf_op jit(solution)/shard_map/ppermute | solution.py:345
  3.3 6.5 %collective-permute-start = (f32[200,128]{1,0:T(8,128)S(1)}, f32[200,128]{1,0:T(8,128)S(1)}, u32[]{:S(2)}, u32[]{:S(2)}) collective-permute-start(f32[200,128]{1,0:T(8,128)S(1)} %pack.1.own_ref), channel_id=1, source_target_pairs={{0,32},{64,96},{128,160},{192,224},{256,288},{320,352},{384,416},{... | collective-permute-start | bytes 307208 | tf_op jit(solution)/shard_map/ppermute | solution.py:345
  10.0 6.0 %collective-permute-start.2 = (f32[96,128]{1,0:T(8,128)S(1)}, f32[96,128]{1,0:T(8,128)S(1)}, u32[]{:S(2)}, u32[]{:S(2)}) collective-permute-start(f32[96,128]{1,0:T(8,128)S(1)} %get-tuple-element.7), channel_id=1, source_target_pairs={{0,1},{2,3},{4,5},{6,7},{8,9},{10,11},{12,13},{14,15},{16,17},{18,... | collective-permute-start | bytes 147464 | tf_op jit(solution)/shard_map/ppermute | solution.py:345
  13.4 2.6 %collective-permute-start.3 = (f32[96,128]{1,0:T(8,128)S(1)}, f32[96,128]{1,0:T(8,128)S(1)}, u32[]{:S(2)}, u32[]{:S(2)}) collective-permute-start(f32[96,128]{1,0:T(8,128)S(1)} %get-tuple-element.8), channel_id=1, source_target_pairs={{1,2},{3,4},{5,6},{7,8},{9,10},{11,12},{13,14},{15,16},{17,18},{19... | collective-permute-start | bytes 147464 | tf_op jit(solution)/shard_map/ppermute | solution.py:345

commit v5 on v4

--- a/solution.py
+++ b/solution.py
@@ -18,7 +18,7 @@
 SLABS = CH * BXC
 FC = SLABS * ROWS
 OWN = FC + ROWS
-EDGE = 3 * SLABS + 3 * ROWS
+EDGE = 3 * SLABS + ROWS
 EXT = 3 * BXC
 step_size = 0.05
 
@@ -61,20 +61,19 @@
     contact_ref,
     sems,
 ):
+    cells = BXC * BLY * BYC
+    parts = [(base_hbm, base_ref, 4), (rate_hbm, rate_ref, 5)]
+    for c in range(4):
+        parts.append((field_hbm.at[pl.ds(c * cells, cells)], field_ref.at[pl.ds(c * cells, cells)], c))
+    contact_copy = pltpu.make_async_copy(contact_hbm, contact_ref, sems.at[6])
+    contact_copy.start()
     copies = [
         pltpu.make_async_copy(source, target, sems.at[n])
-        for n, (source, target) in enumerate(
-            (
-                (contact_hbm, contact_ref),
-                (base_hbm, base_ref),
-                (rate_hbm, rate_ref),
-                (field_hbm, field_ref),
-            )
-        )
+        for n, (source, target, _) in enumerate(parts)
     ]
     for copy in copies:
         copy.start()
-    copies[0].wait()
+    contact_copy.wait()
     row, lane = iotas()
     contact = jnp.zeros((ROWS, LANES), jnp.float32)
     for d in range(6):
@@ -82,11 +81,10 @@
             here = jnp.logical_and(row == block, lane == d)
             contact = jnp.where(here, contact_ref[d, 0, block].astype(jnp.float32), contact)
     own_ref[pl.ds(FC, ROWS), :] = contact
-    for copy in copies[1:]:
+    count = BXC * BLY
+    for copy, (_, ref, channel) in zip(copies, parts):
         copy.wait()
-    first = 0
-    for ref, slabs in ((field_ref, 4 * BXC), (base_ref, BXC), (rate_ref, BXC)):
-        count = slabs * BLY
+        first = channel * BXC
         group = lanes_of(count) // BZC % BLZ
         placed = [None] * BLZ
         for q in range(BLZ):
@@ -98,12 +96,12 @@
                 placed[kz] = moved if q == 0 else jnp.where(group == q, moved, placed[kz])
         for kz in range(BLZ):
             own_ref[pl.ds(first * ROWS + kz, count, stride=BLZ), :] = placed[kz]
-        first += slabs
 
 
 def edge_kernel(own_ref, inside_ref, across_ref, second_ref, first_ref):
     even = lax.axis_index("seg") % 2 == 0
     quarter = lanes_of(SLABS) // (LANES // 4)
+    contact = None
     for part, ref in enumerate((own_ref, inside_ref, across_ref)):
         edges = []
         for jy, start in ((BLY - 1, LANES - LANES // 4), (0, 0)):
@@ -114,11 +112,12 @@
                 edge = moved if kz == 0 else jnp.where(quarter == kz, moved, edge)
             edges.append(edge)
         up, down = edges
-        contact = ref[pl.ds(FC, ROWS), :]
+        faces = lroll(ref[pl.ds(FC, ROWS), :], part * ROWS)
+        contact = faces if part == 0 else contact + faces
         first_ref[pl.ds(part * SLABS, SLABS), :] = jnp.where(even, up, down)
         second_ref[pl.ds(part * SLABS, SLABS), :] = jnp.where(even, down, up)
-        for out_ref in (first_ref, second_ref):
-            out_ref[pl.ds(3 * SLABS + part * ROWS, ROWS), :] = contact
+    for out_ref in (first_ref, second_ref):
+        out_ref[pl.ds(3 * SLABS, ROWS), :] = contact
 
 
 def relax(differences, laplacian, values, base, rate, mix):
@@ -155,6 +154,8 @@
     row, lane = iotas()
     kz, yi, zi = row % BLZ, lane // BZC, lane % BZC
     first_half = row < BLZ
+    up_lane = jnp.where(zi < BZC - 1, lane + 1, lane + 1 - BZC)
+    down_lane = jnp.where(zi > 0, lane - 1, lane + BZC - 1)
     one = jnp.ones((ROWS, LANES), jnp.float32)
     zero = jnp.zeros((ROWS, LANES), jnp.float32)
     total = EXT * CH * RING
@@ -189,14 +190,15 @@
             ring[0, pl.ds(begin + k, SLABS, stride=RING), :] = beyond
             ring[0, pl.ds(begin + k + 3 * BLZ, SLABS, stride=RING), :] = beyond
         contact = ref[pl.ds(FC, ROWS), :]
-        first = first_ref[pl.ds(3 * SLABS + n * ROWS, ROWS), :]
-        second = second_ref[pl.ds(3 * SLABS + n * ROWS, ROWS), :]
+        first = first_ref[pl.ds(3 * SLABS, ROWS), :]
+        second = second_ref[pl.ds(3 * SLABS, ROWS), :]
         faces = []
         beside = sroll(jnp.where(first_half == even_y, first, second), BLZ)
         for d in range(6):
             ab = jnp.broadcast_to(contact[:, d : d + 1], (ROWS, LANES))
             ba = sroll(ab, BLZ)
-            owners = jnp.broadcast_to(beside[:, d : d + 1], (ROWS, LANES))
+            at_lane = n * ROWS + d
+            owners = jnp.broadcast_to(beside[:, at_lane : at_lane + 1], (ROWS, LANES))
             c = jnp.where(lane < LANES // 2, sroll(owners, BLZ), owners)
             ca = jnp.where(first_half, c, ba)
             bc = jnp.where(first_half, ba, sroll(c, BLZ))
@@ -232,17 +234,15 @@
 
             rows = [tile(start + offset[g]) for g in range(3)]
             following, previous = {0: 2, 1: 0, 2: 1}, {0: 1, 1: 2, 2: 0}
-            ups = [lroll(v, -BZC) for v in rows]
-            downs = [lroll(v, BZC) for v in rows]
             for g in groups:
                 v = rows[g]
                 cyl, cyh, nzl, czh, nzh, low, cxl, cxh = coefs[g]
-                n_yh = jnp.where(yi < BYC - 1, ups[g], ups[following[g]])
-                n_yl = jnp.where(yi > 0, downs[g], downs[previous[g]])
-                z_next = lroll(tile(start + offset[g] + 1), BZC - 1)
-                z_last = lroll(tile(start + offset[g] - 1), 1 - BZC)
-                n_zh = jnp.where(zi < BZC - 1, lroll(v, -1), z_next)
-                n_zl = jnp.where(zi > 0, lroll(v, 1), z_last)
+                n_yh = lroll(jnp.where(yi == 0, rows[following[g]], v), -BZC)
+                n_yl = lroll(jnp.where(yi == BYC - 1, rows[previous[g]], v), BZC)
+                z_next = jnp.where(zi == 0, tile(start + offset[g] + 1), v)
+                z_last = jnp.where(zi == BZC - 1, tile(start + offset[g] - 1), v)
+                n_zh = jnp.take_along_axis(z_next, up_lane, axis=1)
+                n_zl = jnp.take_along_axis(z_last, down_lane, axis=1)
                 e_xl = v - tile(before + offset[g])
                 if x == 0:
                     e_xl = cxl * e_xl
@@ -329,7 +329,7 @@
             pltpu.VMEM((BXC * cells, BLZ * BZC), f32),
             pltpu.VMEM((BXC * cells, BLZ * BZC), f32),
             pltpu.SMEM((6, 1, ROWS), jnp.int32),
-            pltpu.SemaphoreType.DMA((4,)),
+            pltpu.SemaphoreType.DMA((7,)),
         ],
         compiler_params=small,
         name="pack",

time: 46.6 us -> 47 us (level)
  Pallas kernels: 4.46 us -> 5.03 us
where the time goes in v5:
time: 47 us; the launch traced here: 46.7 us
  blocking collectives  26.6 us (57%)
  starting transfers between devices  11.6 us (25%)
  Pallas kernels  5.03 us (11%)
  waiting for transfers between devices  2.74 us (6%)
  local copies, waits for them, and re-layouts  0.7 us (1%)
    all_to_all x1, blocking collectives, on_device(): lax.all_to_all(placed.reshape(peers, 4, BXC, LANES), 'seg', split_axis=0,...  26.6 us
    ppermute x4, starting transfers between devices, swap(): return lax.ppermute(value, axis, pairs + [(j, i) for i, j in pairs])  11.6 us
    pallas_call x1, Pallas kernels, on_device(): pl.pallas_call(update_kernel, out_shape=jax.ShapeDtypeStruct((peers, 4 *...  3.06 us
    ppermute x4, waiting for transfers between devices, swap(): return lax.ppermute(value, axis, pairs + [(j, i) for i, j in pairs])  2.74 us
    pallas_call x1, Pallas kernels, on_device(): pl.pallas_call(pack_kernel, out_shape=jax.ShapeDtypeStruct((OWN, LANES),...  1.84 us
  transfers between devices with their start and end apart: 4, of which 2 were waited for; matrix products, arithmetic and copies ran while one was open for 0% of the time, Pallas kernels for 0%

profile of v5, /device:TPU:192, one launch (start us, length us, event | category | flops | bytes accessed | tf_op | source)
XLA Modules:
  0.0 46.7 jit_solution(2876137793438729708)
XLA Ops:
  0.0 1.8 %pack.1.own_ref = f32[200,128]{1,0:T(8,128)S(1)} custom-call(f32[512,32]{1,0:T(8,128)} %bitcast.6, f32[128,32]{1,0:T(8,128)} %bitcast.7, f32[128,32]{1,0:T(8,128)} %bitcast.8, s32[6,1,8]{2,1,0:T(1,128)} %bitcast.9), custom_call_target="tpu_custom_call" | custom-call | tf_op jit(solution)/shard_map/pack/pallas_call | solution.py:322
  1.8 1.9 %collective-permute-start.1 = (f32[200,128]{1,0:T(8,128)S(1)}, f32[200,128]{1,0:T(8,128)S(1)}, u32[]{:S(2)}, u32[]{:S(2)}) collective-permute-start(f32[200,128]{1,0:T(8,128)S(1)} %pack.1.own_ref), channel_id=1, source_target_pairs={{32,64},{96,128},{160,192},{224,256},{288,320},{352,384},{416,448}... | collective-permute-start | bytes 307208 | tf_op jit(solution)/shard_map/ppermute | solution.py:345
  3.8 5.6 %collective-permute-start = (f32[200,128]{1,0:T(8,128)S(1)}, f32[200,128]{1,0:T(8,128)S(1)}, u32[]{:S(2)}, u32[]{:S(2)}) collective-permute-start(f32[200,128]{1,0:T(8,128)S(1)} %pack.1.own_ref), channel_id=1, source_target_pairs={{0,32},{64,96},{128,160},{192,224},{256,288},{320,352},{384,416},{... | collective-permute-start | bytes 307208 | tf_op jit(solution)/shard_map/ppermute | solution.py:345
  9.4 0.0 collective-permute-done.1.across_ref
  9.4 0.9 %collective-permute-done.inside_ref = f32[200,128]{1,0:T(8,128)S(1)} collective-permute-done((f32[200,128]{1,0:T(8,128)S(1)}, f32[200,128]{1,0:T(8,128)S(1)}, u32[]{:S(2)}, u32[]{:S(2)}) %collective-permute-start) | collective-permute-done | bytes 102432 | tf_op jit(solution)/shard_map/ppermute | solution.py:345
  10.3 0.1 edge.1
  10.4 3.4 %collective-permute-start.2 = (f32[80,128]{1,0:T(8,128)S(1)}, f32[80,128]{1,0:T(8,128)S(1)}, u32[]{:S(2)}, u32[]{:S(2)}) collective-permute-start(f32[80,128]{1,0:T(8,128)S(1)} %get-tuple-element.7), channel_id=1, source_target_pairs={{0,1},{2,3},{4,5},{6,7},{8,9},{10,11},{12,13},{14,15},{16,17},{18,... | collective-permute-start | bytes 122888 | tf_op jit(solution)/shard_map/ppermute | solution.py:345
  13.8 0.7 %collective-permute-start.3 = (f32[80,128]{1,0:T(8,128)S(1)}, f32[80,128]{1,0:T(8,128)S(1)}, u32[]{:S(2)}, u32[]{:S(2)}) collective-permute-start(f32[80,128]{1,0:T(8,128)S(1)} %get-tuple-element.8), channel_id=1, source_target_pairs={{1,2},{3,4},{5,6},{7,8},{9,10},{11,12},{13,14},{15,16},{17,18},{19... | collective-permute-start | bytes 122888 | tf_op jit(solution)/shard_map/ppermute | solution.py:345
  14.5 1.8 %collective-permute-done.2.first_ref = f32[80,128]{1,0:T(8,128)S(1)} collective-permute-done((f32[80,128]{1,0:T(8,128)S(1)}, f32[80,128]{1,0:T(8,128)S(1)}, u32[]{:S(2)}, u32[]{:S(2)}) %collective-permute-start.2) | collective-permute-done | bytes 40992 | tf_op jit(solution)/shard_map/ppermute | solution.py:345
  16.3 0.0 collective-permute-done.3.second_ref
  16.3 3.1 %update.1 = f32[32,16,128]{2,1,0:T(8,128)S(1)} custom-call(f32[4,4]{1,0:T(4,128)} %mix_hbm.1, s32[1,8]{1,0:T(1,128)} %owner_hbm.1, f32[200,128]{1,0:T(8,128)S(1)} %pack.1.own_ref, f32[200,128]{1,0:T(8,128)S(1)} %collective-permute-done.inside_ref, f32[200,128]{1,0:T(8,128)S(1)} %collective-permute-done.1.across_ref, ...), custom_call_target="tpu_custom_call" | custom-call | tf_op jit(solution)/shard_map/update/pallas_call | solution.py:362
  19.4 26.6 %all_to_all.5 = f32[32,4,4,128]{3,2,1,0:T(4,128)S(1)} all-to-all(f32[32,4,4,128]{3,2,1,0:T(4,128)S(1)} %bitcast.5), channel_id=1, replica_groups=mesh['grp'=24,'seg'=32] {'seg'}, dimensions={0} | all-to-all | bytes 524288 | tf_op jit(solution)/shard_map/all_to_all | solution.py:378
  46.0 0.7 %copy.8 = f32[32,4,4,128]{3,2,1,0:T(4,128)} copy(f32[32,4,4,128]{3,2,1,0:T(4,128)S(1)} %all_to_all.5) | data formatting | bytes 524288
Async XLA Ops:
  1.8 7.5 %collective-permute-start.1 = (f32[200,128]{1,0:T(8,128)S(1)}, f32[200,128]{1,0:T(8,128)S(1)}, u32[]{:S(2)}, u32[]{:S(2)}) collective-permute-start(f32[200,128]{1,0:T(8,128)S(1)} %pack.1.own_ref), channel_id=1, source_target_pairs={{32,64},{96,128},{160,192},{224,256},{288,320},{352,384},{416,448}... | collective-permute-start | bytes 307208 | tf_op jit(solution)/shard_map/ppermute | solution.py:345
  3.8 6.5 %collective-permute-start = (f32[200,128]{1,0:T(8,128)S(1)}, f32[200,128]{1,0:T(8,128)S(1)}, u32[]{:S(2)}, u32[]{:S(2)}) collective-permute-start(f32[200,128]{1,0:T(8,128)S(1)} %pack.1.own_ref), channel_id=1, source_target_pairs={{0,32},{64,96},{128,160},{192,224},{256,288},{320,352},{384,416},{... | collective-permute-start | bytes 307208 | tf_op jit(solution)/shard_map/ppermute | solution.py:345
  10.4 5.9 %collective-permute-start.2 = (f32[80,128]{1,0:T(8,128)S(1)}, f32[80,128]{1,0:T(8,128)S(1)}, u32[]{:S(2)}, u32[]{:S(2)}) collective-permute-start(f32[80,128]{1,0:T(8,128)S(1)} %get-tuple-element.7), channel_id=1, source_target_pairs={{0,1},{2,3},{4,5},{6,7},{8,9},{10,11},{12,13},{14,15},{16,17},{18,... | collective-permute-start | bytes 122888 | tf_op jit(solution)/shard_map/ppermute | solution.py:345
  13.8 2.5 %collective-permute-start.3 = (f32[80,128]{1,0:T(8,128)S(1)}, f32[80,128]{1,0:T(8,128)S(1)}, u32[]{:S(2)}, u32[]{:S(2)}) collective-permute-start(f32[80,128]{1,0:T(8,128)S(1)} %get-tuple-element.8), channel_id=1, source_target_pairs={{1,2},{3,4},{5,6},{7,8},{9,10},{11,12},{13,14},{15,16},{17,18},{19... | collective-permute-start | bytes 122888 | tf_op jit(solution)/shard_map/ppermute | solution.py:345

commit v6 on v5

--- a/solution.py
+++ b/solution.py
@@ -24,6 +24,7 @@
 
 VMEM = pl.BlockSpec(memory_space=pltpu.VMEM)
 SMEM = pl.BlockSpec(memory_space=pltpu.SMEM)
+ANY = pl.BlockSpec(memory_space=pl.ANY)
 HBM = pl.BlockSpec(memory_space=pltpu.HBM)
 
 
@@ -61,19 +62,20 @@
     contact_ref,
     sems,
 ):
-    cells = BXC * BLY * BYC
-    parts = [(base_hbm, base_ref, 4), (rate_hbm, rate_ref, 5)]
-    for c in range(4):
-        parts.append((field_hbm.at[pl.ds(c * cells, cells)], field_ref.at[pl.ds(c * cells, cells)], c))
-    contact_copy = pltpu.make_async_copy(contact_hbm, contact_ref, sems.at[6])
-    contact_copy.start()
     copies = [
         pltpu.make_async_copy(source, target, sems.at[n])
-        for n, (source, target, _) in enumerate(parts)
+        for n, (source, target) in enumerate(
+            (
+                (contact_hbm, contact_ref),
+                (base_hbm, base_ref),
+                (rate_hbm, rate_ref),
+                (field_hbm, field_ref),
+            )
+        )
     ]
     for copy in copies:
         copy.start()
-    contact_copy.wait()
+    copies[0].wait()
     row, lane = iotas()
     contact = jnp.zeros((ROWS, LANES), jnp.float32)
     for d in range(6):
@@ -81,10 +83,11 @@
             here = jnp.logical_and(row == block, lane == d)
             contact = jnp.where(here, contact_ref[d, 0, block].astype(jnp.float32), contact)
     own_ref[pl.ds(FC, ROWS), :] = contact
-    count = BXC * BLY
-    for copy, (_, ref, channel) in zip(copies, parts):
+    for copy in copies[1:]:
         copy.wait()
-        first = channel * BXC
+    first = 0
+    for ref, slabs in ((field_ref, 4 * BXC), (base_ref, BXC), (rate_ref, BXC)):
+        count = slabs * BLY
         group = lanes_of(count) // BZC % BLZ
         placed = [None] * BLZ
         for q in range(BLZ):
@@ -96,6 +99,7 @@
                 placed[kz] = moved if q == 0 else jnp.where(group == q, moved, placed[kz])
         for kz in range(BLZ):
             own_ref[pl.ds(first * ROWS + kz, count, stride=BLZ), :] = placed[kz]
+        first += slabs
 
 
 def edge_kernel(own_ref, inside_ref, across_ref, second_ref, first_ref):
@@ -329,7 +333,7 @@
             pltpu.VMEM((BXC * cells, BLZ * BZC), f32),
             pltpu.VMEM((BXC * cells, BLZ * BZC), f32),
             pltpu.SMEM((6, 1, ROWS), jnp.int32),
-            pltpu.SemaphoreType.DMA((7,)),
+            pltpu.SemaphoreType.DMA((4,)),
         ],
         compiler_params=small,
         name="pack",
@@ -362,7 +366,7 @@
     placed = pl.pallas_call(
         update_kernel,
         out_shape=jax.ShapeDtypeStruct((peers, 4 * BXC, LANES), f32),
-        in_specs=[HBM, HBM] + [VMEM] * 5,
+        in_specs=[ANY, ANY] + [VMEM] * 5,
         out_specs=VMEM,
         scratch_shapes=[
             pltpu.VMEM((2, EXT * CH * RING + 2 * PAD, LANES), f32),
@@ -374,7 +378,7 @@
         ],
         compiler_params=pltpu.CompilerParams(vmem_limit_bytes=8 << 20),
         name="update",
-    )(in_hbm(mixing), in_hbm(new_owner), own, inside, across, first, second)
+    )(mixing, new_owner, own, inside, across, first, second)
     received = lax.all_to_all(
         placed.reshape(peers, 4, BXC, LANES), "seg", split_axis=0, concat_axis=0, tiled=True
     )

time: 47 us -> 46.3 us (0.985)
  Pallas kernels: 5.03 us -> 4.33 us
where the time goes in v6:
time: 46.3 us; the launch traced here: 46.1 us
  blocking collectives  26.6 us (57%)
  starting transfers between devices  11.6 us (25%)
  Pallas kernels  4.33 us (9%)
  waiting for transfers between devices  2.74 us (6%)
  local copies, waits for them, and re-layouts  0.72 us (2%)
    all_to_all x1, blocking collectives, on_device(): lax.all_to_all(placed.reshape(peers, 4, BXC, LANES), 'seg', split_axis=0,...  26.6 us
    ppermute x4, starting transfers between devices, swap(): return lax.ppermute(value, axis, pairs + [(j, i) for i, j in pairs])  11.6 us
    pallas_call x1, Pallas kernels, on_device(): pl.pallas_call(update_kernel, out_shape=jax.ShapeDtypeStruct((peers, 4 *...  2.82 us
    ppermute x4, waiting for transfers between devices, swap(): return lax.ppermute(value, axis, pairs + [(j, i) for i, j in pairs])  2.74 us
    pallas_call x1, Pallas kernels, on_device(): pl.pallas_call(pack_kernel, out_shape=jax.ShapeDtypeStruct((OWN, LANES),...  1.39 us
  transfers between devices with their start and end apart: 4, of which 2 were waited for; matrix products, arithmetic and copies ran while one was open for 0% of the time, Pallas kernels for 0%

profile of v6, /device:TPU:192, one launch (start us, length us, event | category | flops | bytes accessed | tf_op | source)
XLA Modules:
  0.0 46.1 jit_solution(10245879287724523310)
XLA Ops:
  0.0 1.4 %pack.1.own_ref = f32[200,128]{1,0:T(8,128)S(1)} custom-call(f32[512,32]{1,0:T(8,128)} %bitcast.6, f32[128,32]{1,0:T(8,128)} %bitcast.7, f32[128,32]{1,0:T(8,128)} %bitcast.8, s32[6,1,8]{2,1,0:T(1,128)} %bitcast.9), custom_call_target="tpu_custom_call" | custom-call | tf_op jit(solution)/shard_map/pack/pallas_call | solution.py:326
  1.4 1.9 %collective-permute-start.1 = (f32[200,128]{1,0:T(8,128)S(1)}, f32[200,128]{1,0:T(8,128)S(1)}, u32[]{:S(2)}, u32[]{:S(2)}) collective-permute-start(f32[200,128]{1,0:T(8,128)S(1)} %pack.1.own_ref), channel_id=1, source_target_pairs={{32,64},{96,128},{160,192},{224,256},{288,320},{352,384},{416,448}... | collective-permute-start | bytes 307208 | tf_op jit(solution)/shard_map/ppermute | solution.py:349
  3.3 5.6 %collective-permute-start = (f32[200,128]{1,0:T(8,128)S(1)}, f32[200,128]{1,0:T(8,128)S(1)}, u32[]{:S(2)}, u32[]{:S(2)}) collective-permute-start(f32[200,128]{1,0:T(8,128)S(1)} %pack.1.own_ref), channel_id=1, source_target_pairs={{0,32},{64,96},{128,160},{192,224},{256,288},{320,352},{384,416},{... | collective-permute-start | bytes 307208 | tf_op jit(solution)/shard_map/ppermute | solution.py:349
  8.9 0.0 collective-permute-done.1.across_ref
  8.9 0.9 %collective-permute-done.inside_ref = f32[200,128]{1,0:T(8,128)S(1)} collective-permute-done((f32[200,128]{1,0:T(8,128)S(1)}, f32[200,128]{1,0:T(8,128)S(1)}, u32[]{:S(2)}, u32[]{:S(2)}) %collective-permute-start) | collective-permute-done | bytes 102432 | tf_op jit(solution)/shard_map/ppermute | solution.py:349
  9.9 0.1 edge.1
  10.0 0.0 copy-start
  10.0 0.0 copy-start.1
  10.0 3.4 %collective-permute-start.2 = (f32[80,128]{1,0:T(8,128)S(1)}, f32[80,128]{1,0:T(8,128)S(1)}, u32[]{:S(2)}, u32[]{:S(2)}) collective-permute-start(f32[80,128]{1,0:T(8,128)S(1)} %get-tuple-element.7), channel_id=1, source_target_pairs={{0,1},{2,3},{4,5},{6,7},{8,9},{10,11},{12,13},{14,15},{16,17},{18,... | collective-permute-start | bytes 122888 | tf_op jit(solution)/shard_map/ppermute | solution.py:349
  13.4 0.7 %collective-permute-start.3 = (f32[80,128]{1,0:T(8,128)S(1)}, f32[80,128]{1,0:T(8,128)S(1)}, u32[]{:S(2)}, u32[]{:S(2)}) collective-permute-start(f32[80,128]{1,0:T(8,128)S(1)} %get-tuple-element.8), channel_id=1, source_target_pairs={{1,2},{3,4},{5,6},{7,8},{9,10},{11,12},{13,14},{15,16},{17,18},{19... | collective-permute-start | bytes 122888 | tf_op jit(solution)/shard_map/ppermute | solution.py:349
  14.1 1.8 %collective-permute-done.2.first_ref = f32[80,128]{1,0:T(8,128)S(1)} collective-permute-done((f32[80,128]{1,0:T(8,128)S(1)}, f32[80,128]{1,0:T(8,128)S(1)}, u32[]{:S(2)}, u32[]{:S(2)}) %collective-permute-start.2) | collective-permute-done | bytes 40992 | tf_op jit(solution)/shard_map/ppermute | solution.py:349
  15.9 0.0 collective-permute-done.3.second_ref
  15.9 0.0 copy-done
  15.9 0.0 copy-done.1
  15.9 2.8 %update.1 = f32[32,16,128]{2,1,0:T(8,128)S(1)} custom-call(f32[4,4]{1,0:T(4,128)S(1)} %copy-done, s32[1,8]{1,0:T(1,128)S(1)} %copy-done.1, f32[200,128]{1,0:T(8,128)S(1)} %pack.1.own_ref, f32[200,128]{1,0:T(8,128)S(1)} %collective-permute-done.inside_ref, f32[200,128]{1,0:T(8,128)S(1)} %collective-permute-done.1.across_ref, ...), custom_call_target="tpu_custom_call" | custom-call | tf_op jit(solution)/shard_map/update/pallas_call | solution.py:366
  18.7 26.6 %all_to_all.5 = f32[32,4,4,128]{3,2,1,0:T(4,128)S(1)} all-to-all(f32[32,4,4,128]{3,2,1,0:T(4,128)S(1)} %bitcast.5), channel_id=1, replica_groups=mesh['grp'=24,'seg'=32] {'seg'}, dimensions={0} | all-to-all | bytes 524288 | tf_op jit(solution)/shard_map/all_to_all | solution.py:382
  45.4 0.7 %copy.8 = f32[32,4,4,128]{3,2,1,0:T(4,128)} copy(f32[32,4,4,128]{3,2,1,0:T(4,128)S(1)} %all_to_all.5) | data formatting | bytes 524288
Async XLA Ops:
  1.4 7.5 %collective-permute-start.1 = (f32[200,128]{1,0:T(8,128)S(1)}, f32[200,128]{1,0:T(8,128)S(1)}, u32[]{:S(2)}, u32[]{:S(2)}) collective-permute-start(f32[200,128]{1,0:T(8,128)S(1)} %pack.1.own_ref), channel_id=1, source_target_pairs={{32,64},{96,128},{160,192},{224,256},{288,320},{352,384},{416,448}... | collective-permute-start | bytes 307208 | tf_op jit(solution)/shard_map/ppermute | solution.py:349
  3.3 6.5 %collective-permute-start = (f32[200,128]{1,0:T(8,128)S(1)}, f32[200,128]{1,0:T(8,128)S(1)}, u32[]{:S(2)}, u32[]{:S(2)}) collective-permute-start(f32[200,128]{1,0:T(8,128)S(1)} %pack.1.own_ref), channel_id=1, source_target_pairs={{0,32},{64,96},{128,160},{192,224},{256,288},{320,352},{384,416},{... | collective-permute-start | bytes 307208 | tf_op jit(solution)/shard_map/ppermute | solution.py:349
  10.0 5.9 %copy-start = (f32[4,4]{1,0:T(4,128)S(1)}, f32[4,4]{1,0:T(4,128)}, u32[]{:S(2)}) copy-start(f32[4,4]{1,0:T(4,128)} %mix_hbm.1) | copy-start | bytes 196
  10.0 5.9 %copy-start.1 = (s32[1,8]{1,0:T(1,128)S(1)}, s32[1,8]{1,0:T(1,128)}, u32[]{:S(2)}) copy-start(s32[1,8]{1,0:T(1,128)} %owner_hbm.1) | copy-start | bytes 100
  10.0 5.9 %collective-permute-start.2 = (f32[80,128]{1,0:T(8,128)S(1)}, f32[80,128]{1,0:T(8,128)S(1)}, u32[]{:S(2)}, u32[]{:S(2)}) collective-permute-start(f32[80,128]{1,0:T(8,128)S(1)} %get-tuple-element.7), channel_id=1, source_target_pairs={{0,1},{2,3},{4,5},{6,7},{8,9},{10,11},{12,13},{14,15},{16,17},{18,... | collective-permute-start | bytes 122888 | tf_op jit(solution)/shard_map/ppermute | solution.py:349
  13.4 2.5 %collective-permute-start.3 = (f32[80,128]{1,0:T(8,128)S(1)}, f32[80,128]{1,0:T(8,128)S(1)}, u32[]{:S(2)}, u32[]{:S(2)}) collective-permute-start(f32[80,128]{1,0:T(8,128)S(1)} %get-tuple-element.8), channel_id=1, source_target_pairs={{1,2},{3,4},{5,6},{7,8},{9,10},{11,12},{13,14},{15,16},{17,18},{19... | collective-permute-start | bytes 122888 | tf_op jit(solution)/shard_map/ppermute | solution.py:349

commit v7 on v6

--- a/solution.py
+++ b/solution.py
@@ -170,9 +170,11 @@
     for now in range(2):
         ring[now, pl.ds(0, PAD), :] = zero
         ring[now, pl.ds(PAD + total, PAD), :] = zero
-    for i, channel in ((0, 1), (0, 2), (0, 3), (0, 4), (BXC, 4)):
+    above = [(0, 1), (0, 2), (0, 3), (0, 4), (BXC, 4)] + [(EXT - 2, c) for c in range(4)]
+    for i, channel in above:
         ring[1, pl.ds(at(i, channel), ROWS), :] = zero
-    for i, channel in ((BXC - 1, 5), (2 * BXC - 1, 5), (EXT - 1, 0), (EXT - 1, 1), (EXT - 1, 2)):
+    below = [(BXC - 1, 5), (2 * BXC - 1, 5), (EXT - 1, 0), (EXT - 1, 1), (EXT - 1, 2)]
+    for i, channel in below + [(1, c) for c in range(4)]:
         ring[1, pl.ds(at(i, channel) + ROWS, ROWS), :] = zero
     for n, ref in enumerate((own_ref, inside_ref, across_ref)):
         part = places[n]
@@ -222,9 +224,10 @@
     def put(now, start, value):
         ring[now, pl.ds(start, ROWS), :] = value
 
-    def sweep(now, i, last):
+    def sweep(now, i, last, step):
         part, x = i // BXC, i % BXC
-        groups = (2,) if last else (0, 1)
+        alone = last or i in (step + 1, EXT - 2 - step)
+        groups = (2,) if alone else (0, 1)
         offset = {0: 0, 1: ROWS, 2: BLZ}
         coefs = {g: [cin[part, g, d] for d in range(8)] for g in groups}
         laps = {g: [] for g in groups}
@@ -279,7 +282,7 @@
     state = [None] * BXC
     for step in range(STEPS1):
         for i in range(step + 1, EXT - 1 - step):
-            sweep(step % 2, i, step == STEPS1 - 1)
+            sweep(step % 2, i, step == STEPS1 - 1, step)
 
     y_inner = jnp.where(yi < BYC - 1, 1.0, 0.0)
     z_inner = jnp.where(zi < BZC - 1, 1.0, 0.0)

time: 46.3 us -> 46.2 us (level)
  no operation moved by 1% of the time
where the time goes in v7:
time: 46.2 us; the launch traced here: 45.9 us
  blocking collectives  26.6 us (58%)
  starting transfers between devices  11.6 us (25%)
  Pallas kernels  4.16 us (9%)
  waiting for transfers between devices  2.74 us (6%)
  local copies, waits for them, and re-layouts  0.72 us (2%)
    all_to_all x1, blocking collectives, on_device(): lax.all_to_all(placed.reshape(peers, 4, BXC, LANES), 'seg', split_axis=0,...  26.6 us
    ppermute x4, starting transfers between devices, swap(): return lax.ppermute(value, axis, pairs + [(j, i) for i, j in pairs])  11.6 us
    ppermute x4, waiting for transfers between devices, swap(): return lax.ppermute(value, axis, pairs + [(j, i) for i, j in pairs])  2.74 us
    pallas_call x1, Pallas kernels, on_device(): pl.pallas_call(update_kernel, out_shape=jax.ShapeDtypeStruct((peers, 4 *...  2.65 us
    pallas_call x1, Pallas kernels, on_device(): pl.pallas_call(pack_kernel, out_shape=jax.ShapeDtypeStruct((OWN, LANES),...  1.39 us
  transfers between devices with their start and end apart: 4, of which 2 were waited for; matrix products, arithmetic and copies ran while one was open for 0% of the time, Pallas kernels for 0%

profile of v7, /device:TPU:192, one launch (start us, length us, event | category | flops | bytes accessed | tf_op | source)
XLA Modules:
  0.0 45.9 jit_solution(13373385523213895809)
XLA Ops:
  0.0 1.4 %pack.1.own_ref = f32[200,128]{1,0:T(8,128)S(1)} custom-call(f32[512,32]{1,0:T(8,128)} %bitcast.6, f32[128,32]{1,0:T(8,128)} %bitcast.7, f32[128,32]{1,0:T(8,128)} %bitcast.8, s32[6,1,8]{2,1,0:T(1,128)} %bitcast.9), custom_call_target="tpu_custom_call" | custom-call | tf_op jit(solution)/shard_map/pack/pallas_call | solution.py:329
  1.4 1.9 %collective-permute-start.1 = (f32[200,128]{1,0:T(8,128)S(1)}, f32[200,128]{1,0:T(8,128)S(1)}, u32[]{:S(2)}, u32[]{:S(2)}) collective-permute-start(f32[200,128]{1,0:T(8,128)S(1)} %pack.1.own_ref), channel_id=1, source_target_pairs={{32,64},{96,128},{160,192},{224,256},{288,320},{352,384},{416,448}... | collective-permute-start | bytes 307208 | tf_op jit(solution)/shard_map/ppermute | solution.py:352
  3.3 5.6 %collective-permute-start = (f32[200,128]{1,0:T(8,128)S(1)}, f32[200,128]{1,0:T(8,128)S(1)}, u32[]{:S(2)}, u32[]{:S(2)}) collective-permute-start(f32[200,128]{1,0:T(8,128)S(1)} %pack.1.own_ref), channel_id=1, source_target_pairs={{0,32},{64,96},{128,160},{192,224},{256,288},{320,352},{384,416},{... | collective-permute-start | bytes 307208 | tf_op jit(solution)/shard_map/ppermute | solution.py:352
  8.9 0.0 collective-permute-done.1.across_ref
  8.9 0.9 %collective-permute-done.inside_ref = f32[200,128]{1,0:T(8,128)S(1)} collective-permute-done((f32[200,128]{1,0:T(8,128)S(1)}, f32[200,128]{1,0:T(8,128)S(1)}, u32[]{:S(2)}, u32[]{:S(2)}) %collective-permute-start) | collective-permute-done | bytes 102432 | tf_op jit(solution)/shard_map/ppermute | solution.py:352
  9.9 0.1 edge.1
  10.0 0.0 copy-start
  10.0 0.0 copy-start.1
  10.0 3.4 %collective-permute-start.2 = (f32[80,128]{1,0:T(8,128)S(1)}, f32[80,128]{1,0:T(8,128)S(1)}, u32[]{:S(2)}, u32[]{:S(2)}) collective-permute-start(f32[80,128]{1,0:T(8,128)S(1)} %get-tuple-element.7), channel_id=1, source_target_pairs={{0,1},{2,3},{4,5},{6,7},{8,9},{10,11},{12,13},{14,15},{16,17},{18,... | collective-permute-start | bytes 122888 | tf_op jit(solution)/shard_map/ppermute | solution.py:352
  13.4 0.7 %collective-permute-start.3 = (f32[80,128]{1,0:T(8,128)S(1)}, f32[80,128]{1,0:T(8,128)S(1)}, u32[]{:S(2)}, u32[]{:S(2)}) collective-permute-start(f32[80,128]{1,0:T(8,128)S(1)} %get-tuple-element.8), channel_id=1, source_target_pairs={{1,2},{3,4},{5,6},{7,8},{9,10},{11,12},{13,14},{15,16},{17,18},{19... | collective-permute-start | bytes 122888 | tf_op jit(solution)/shard_map/ppermute | solution.py:352
  14.1 1.8 %collective-permute-done.2.first_ref = f32[80,128]{1,0:T(8,128)S(1)} collective-permute-done((f32[80,128]{1,0:T(8,128)S(1)}, f32[80,128]{1,0:T(8,128)S(1)}, u32[]{:S(2)}, u32[]{:S(2)}) %collective-permute-start.2) | collective-permute-done | bytes 40992 | tf_op jit(solution)/shard_map/ppermute | solution.py:352
  15.9 0.0 collective-permute-done.3.second_ref
  15.9 0.0 copy-done
  15.9 0.0 copy-done.1
  15.9 2.6 %update.1 = f32[32,16,128]{2,1,0:T(8,128)S(1)} custom-call(f32[4,4]{1,0:T(4,128)S(1)} %copy-done, s32[1,8]{1,0:T(1,128)S(1)} %copy-done.1, f32[200,128]{1,0:T(8,128)S(1)} %pack.1.own_ref, f32[200,128]{1,0:T(8,128)S(1)} %collective-permute-done.inside_ref, f32[200,128]{1,0:T(8,128)S(1)} %collective-permute-done.1.across_ref, ...), custom_call_target="tpu_custom_call" | custom-call | tf_op jit(solution)/shard_map/update/pallas_call | solution.py:369
  18.6 26.6 %all_to_all.5 = f32[32,4,4,128]{3,2,1,0:T(4,128)S(1)} all-to-all(f32[32,4,4,128]{3,2,1,0:T(4,128)S(1)} %bitcast.5), channel_id=1, replica_groups=mesh['grp'=24,'seg'=32] {'seg'}, dimensions={0} | all-to-all | bytes 524288 | tf_op jit(solution)/shard_map/all_to_all | solution.py:385
  45.2 0.7 %copy.8 = f32[32,4,4,128]{3,2,1,0:T(4,128)} copy(f32[32,4,4,128]{3,2,1,0:T(4,128)S(1)} %all_to_all.5) | data formatting | bytes 524288
Async XLA Ops:
  1.4 7.5 %collective-permute-start.1 = (f32[200,128]{1,0:T(8,128)S(1)}, f32[200,128]{1,0:T(8,128)S(1)}, u32[]{:S(2)}, u32[]{:S(2)}) collective-permute-start(f32[200,128]{1,0:T(8,128)S(1)} %pack.1.own_ref), channel_id=1, source_target_pairs={{32,64},{96,128},{160,192},{224,256},{288,320},{352,384},{416,448}... | collective-permute-start | bytes 307208 | tf_op jit(solution)/shard_map/ppermute | solution.py:352
  3.3 6.5 %collective-permute-start = (f32[200,128]{1,0:T(8,128)S(1)}, f32[200,128]{1,0:T(8,128)S(1)}, u32[]{:S(2)}, u32[]{:S(2)}) collective-permute-start(f32[200,128]{1,0:T(8,128)S(1)} %pack.1.own_ref), channel_id=1, source_target_pairs={{0,32},{64,96},{128,160},{192,224},{256,288},{320,352},{384,416},{... | collective-permute-start | bytes 307208 | tf_op jit(solution)/shard_map/ppermute | solution.py:352
  10.0 5.9 %copy-start = (f32[4,4]{1,0:T(4,128)S(1)}, f32[4,4]{1,0:T(4,128)}, u32[]{:S(2)}) copy-start(f32[4,4]{1,0:T(4,128)} %mix_hbm.1) | copy-start | bytes 196
  10.0 5.9 %copy-start.1 = (s32[1,8]{1,0:T(1,128)S(1)}, s32[1,8]{1,0:T(1,128)}, u32[]{:S(2)}) copy-start(s32[1,8]{1,0:T(1,128)} %owner_hbm.1) | copy-start | bytes 100
  10.0 5.9 %collective-permute-start.2 = (f32[80,128]{1,0:T(8,128)S(1)}, f32[80,128]{1,0:T(8,128)S(1)}, u32[]{:S(2)}, u32[]{:S(2)}) collective-permute-start(f32[80,128]{1,0:T(8,128)S(1)} %get-tuple-element.7), channel_id=1, source_target_pairs={{0,1},{2,3},{4,5},{6,7},{8,9},{10,11},{12,13},{14,15},{16,17},{18,... | collective-permute-start | bytes 122888 | tf_op jit(solution)/shard_map/ppermute | solution.py:352
  13.4 2.5 %collective-permute-start.3 = (f32[80,128]{1,0:T(8,128)S(1)}, f32[80,128]{1,0:T(8,128)S(1)}, u32[]{:S(2)}, u32[]{:S(2)}) collective-permute-start(f32[80,128]{1,0:T(8,128)S(1)} %get-tuple-element.8), channel_id=1, source_target_pairs={{1,2},{3,4},{5,6},{7,8},{9,10},{11,12},{13,14},{15,16},{17,18},{19... | collective-permute-start | bytes 122888 | tf_op jit(solution)/shard_map/ppermute | solution.py:352

commit v8 on v7

--- a/solution.py
+++ b/solution.py
@@ -289,7 +289,8 @@
     y_low_inner = jnp.where(yi > 0, 1.0, 0.0)
     z_low_inner = jnp.where(zi > 0, 1.0, 0.0)
     out_ref[...] = jnp.zeros_like(out_ref)
-    for _ in range(STEPS2):
+
+    def settle(_, state):
         fresh = []
         rise = [[state[x + 1][c] - state[x][c] for c in range(4)] for x in range(BXC - 1)]
         rise.append([zero] * 4)
@@ -313,7 +314,9 @@
             base = ring[0, pl.ds(at(BXC + x, 4) + BLZ, ROWS), :] * step_size
             rate = ring[0, pl.ds(at(BXC + x, 5) + BLZ, ROWS), :]
             fresh.append(relax(diffs, laps, state[x], base, rate, mix))
-        state = fresh
+        return fresh
+
+    state = lax.fori_loop(0, STEPS2, settle, state)
     for x in range(BXC):
         for c in range(4):
             done[pl.ds((c * BXC + x) * ROWS, ROWS), :] = state[x][c]

time: 46.2 us -> 46.3 us (level)
  no operation moved by 1% of the time
where the time goes in v8:
time: 46.3 us; the launch traced here: 46 us
  blocking collectives  26.6 us (57%)
  starting transfers between devices  11.6 us (25%)
  Pallas kernels  4.28 us (9%)
  waiting for transfers between devices  2.74 us (6%)
  local copies, waits for them, and re-layouts  0.72 us (2%)
    all_to_all x1, blocking collectives, on_device(): lax.all_to_all(placed.reshape(peers, 4, BXC, LANES), 'seg', split_axis=0,...  26.6 us
    ppermute x4, starting transfers between devices, swap(): return lax.ppermute(value, axis, pairs + [(j, i) for i, j in pairs])  11.6 us
    pallas_call x1, Pallas kernels, on_device(): pl.pallas_call(update_kernel, out_shape=jax.ShapeDtypeStruct((peers, 4 *...  2.77 us
    ppermute x4, waiting for transfers between devices, swap(): return lax.ppermute(value, axis, pairs + [(j, i) for i, j in pairs])  2.74 us
    pallas_call x1, Pallas kernels, on_device(): pl.pallas_call(pack_kernel, out_shape=jax.ShapeDtypeStruct((OWN, LANES),...  1.39 us
  transfers between devices with their start and end apart: 4, of which 2 were waited for; matrix products, arithmetic and copies ran while one was open for 0% of the time, Pallas kernels for 0%

profile of v8, /device:TPU:192, one launch (start us, length us, event | category | flops | bytes accessed | tf_op | source)
XLA Modules:
  0.0 46.0 jit_solution(3748778803277019743)
XLA Ops:
  0.0 1.4 %pack.1.own_ref = f32[200,128]{1,0:T(8,128)S(1)} custom-call(f32[512,32]{1,0:T(8,128)} %bitcast.6, f32[128,32]{1,0:T(8,128)} %bitcast.7, f32[128,32]{1,0:T(8,128)} %bitcast.8, s32[6,1,8]{2,1,0:T(1,128)} %bitcast.9), custom_call_target="tpu_custom_call" | custom-call | tf_op jit(solution)/shard_map/pack/pallas_call | solution.py:332
  1.4 1.9 %collective-permute-start.1 = (f32[200,128]{1,0:T(8,128)S(1)}, f32[200,128]{1,0:T(8,128)S(1)}, u32[]{:S(2)}, u32[]{:S(2)}) collective-permute-start(f32[200,128]{1,0:T(8,128)S(1)} %pack.1.own_ref), channel_id=1, source_target_pairs={{32,64},{96,128},{160,192},{224,256},{288,320},{352,384},{416,448}... | collective-permute-start | bytes 307208 | tf_op jit(solution)/shard_map/ppermute | solution.py:355
  3.3 5.6 %collective-permute-start = (f32[200,128]{1,0:T(8,128)S(1)}, f32[200,128]{1,0:T(8,128)S(1)}, u32[]{:S(2)}, u32[]{:S(2)}) collective-permute-start(f32[200,128]{1,0:T(8,128)S(1)} %pack.1.own_ref), channel_id=1, source_target_pairs={{0,32},{64,96},{128,160},{192,224},{256,288},{320,352},{384,416},{... | collective-permute-start | bytes 307208 | tf_op jit(solution)/shard_map/ppermute | solution.py:355
  8.9 0.0 collective-permute-done.1.across_ref
  8.9 0.9 %collective-permute-done.inside_ref = f32[200,128]{1,0:T(8,128)S(1)} collective-permute-done((f32[200,128]{1,0:T(8,128)S(1)}, f32[200,128]{1,0:T(8,128)S(1)}, u32[]{:S(2)}, u32[]{:S(2)}) %collective-permute-start) | collective-permute-done | bytes 102432 | tf_op jit(solution)/shard_map/ppermute | solution.py:355
  9.9 0.1 edge.1
  10.0 0.0 copy-start
  10.0 0.0 copy-start.1
  10.0 3.4 %collective-permute-start.2 = (f32[80,128]{1,0:T(8,128)S(1)}, f32[80,128]{1,0:T(8,128)S(1)}, u32[]{:S(2)}, u32[]{:S(2)}) collective-permute-start(f32[80,128]{1,0:T(8,128)S(1)} %get-tuple-element.7), channel_id=1, source_target_pairs={{0,1},{2,3},{4,5},{6,7},{8,9},{10,11},{12,13},{14,15},{16,17},{18,... | collective-permute-start | bytes 122888 | tf_op jit(solution)/shard_map/ppermute | solution.py:355
  13.4 0.7 %collective-permute-start.3 = (f32[80,128]{1,0:T(8,128)S(1)}, f32[80,128]{1,0:T(8,128)S(1)}, u32[]{:S(2)}, u32[]{:S(2)}) collective-permute-start(f32[80,128]{1,0:T(8,128)S(1)} %get-tuple-element.8), channel_id=1, source_target_pairs={{1,2},{3,4},{5,6},{7,8},{9,10},{11,12},{13,14},{15,16},{17,18},{19... | collective-permute-start | bytes 122888 | tf_op jit(solution)/shard_map/ppermute | solution.py:355
  14.1 1.8 %collective-permute-done.2.first_ref = f32[80,128]{1,0:T(8,128)S(1)} collective-permute-done((f32[80,128]{1,0:T(8,128)S(1)}, f32[80,128]{1,0:T(8,128)S(1)}, u32[]{:S(2)}, u32[]{:S(2)}) %collective-permute-start.2) | collective-permute-done | bytes 40992 | tf_op jit(solution)/shard_map/ppermute | solution.py:355
  15.9 0.0 collective-permute-done.3.second_ref
  15.9 0.0 copy-done
  15.9 0.0 copy-done.1
  15.9 2.8 %update.1 = f32[32,16,128]{2,1,0:T(8,128)S(1)} custom-call(f32[4,4]{1,0:T(4,128)S(1)} %copy-done, s32[1,8]{1,0:T(1,128)S(1)} %copy-done.1, f32[200,128]{1,0:T(8,128)S(1)} %pack.1.own_ref, f32[200,128]{1,0:T(8,128)S(1)} %collective-permute-done.inside_ref, f32[200,128]{1,0:T(8,128)S(1)} %collective-permute-done.1.across_ref, ...), custom_call_target="tpu_custom_call" | custom-call | tf_op jit(solution)/shard_map/update/pallas_call | solution.py:372
  18.7 26.6 %all_to_all.5 = f32[32,4,4,128]{3,2,1,0:T(4,128)S(1)} all-to-all(f32[32,4,4,128]{3,2,1,0:T(4,128)S(1)} %bitcast.5), channel_id=1, replica_groups=mesh['grp'=24,'seg'=32] {'seg'}, dimensions={0} | all-to-all | bytes 524288 | tf_op jit(solution)/shard_map/all_to_all | solution.py:388
  45.3 0.7 %copy.8 = f32[32,4,4,128]{3,2,1,0:T(4,128)} copy(f32[32,4,4,128]{3,2,1,0:T(4,128)S(1)} %all_to_all.5) | data formatting | bytes 524288
Async XLA Ops:
  1.4 7.5 %collective-permute-start.1 = (f32[200,128]{1,0:T(8,128)S(1)}, f32[200,128]{1,0:T(8,128)S(1)}, u32[]{:S(2)}, u32[]{:S(2)}) collective-permute-start(f32[200,128]{1,0:T(8,128)S(1)} %pack.1.own_ref), channel_id=1, source_target_pairs={{32,64},{96,128},{160,192},{224,256},{288,320},{352,384},{416,448}... | collective-permute-start | bytes 307208 | tf_op jit(solution)/shard_map/ppermute | solution.py:355
  3.3 6.5 %collective-permute-start = (f32[200,128]{1,0:T(8,128)S(1)}, f32[200,128]{1,0:T(8,128)S(1)}, u32[]{:S(2)}, u32[]{:S(2)}) collective-permute-start(f32[200,128]{1,0:T(8,128)S(1)} %pack.1.own_ref), channel_id=1, source_target_pairs={{0,32},{64,96},{128,160},{192,224},{256,288},{320,352},{384,416},{... | collective-permute-start | bytes 307208 | tf_op jit(solution)/shard_map/ppermute | solution.py:355
  10.0 5.9 %copy-start = (f32[4,4]{1,0:T(4,128)S(1)}, f32[4,4]{1,0:T(4,128)}, u32[]{:S(2)}) copy-start(f32[4,4]{1,0:T(4,128)} %mix_hbm.1) | copy-start | bytes 196
  10.0 5.9 %copy-start.1 = (s32[1,8]{1,0:T(1,128)S(1)}, s32[1,8]{1,0:T(1,128)}, u32[]{:S(2)}) copy-start(s32[1,8]{1,0:T(1,128)} %owner_hbm.1) | copy-start | bytes 100
  10.0 5.9 %collective-permute-start.2 = (f32[80,128]{1,0:T(8,128)S(1)}, f32[80,128]{1,0:T(8,128)S(1)}, u32[]{:S(2)}, u32[]{:S(2)}) collective-permute-start(f32[80,128]{1,0:T(8,128)S(1)} %get-tuple-element.7), channel_id=1, source_target_pairs={{0,1},{2,3},{4,5},{6,7},{8,9},{10,11},{12,13},{14,15},{16,17},{18,... | collective-permute-start | bytes 122888 | tf_op jit(solution)/shard_map/ppermute | solution.py:355
  13.4 2.5 %collective-permute-start.3 = (f32[80,128]{1,0:T(8,128)S(1)}, f32[80,128]{1,0:T(8,128)S(1)}, u32[]{:S(2)}, u32[]{:S(2)}) collective-permute-start(f32[80,128]{1,0:T(8,128)S(1)} %get-tuple-element.8), channel_id=1, source_target_pairs={{1,2},{3,4},{5,6},{7,8},{9,10},{11,12},{13,14},{15,16},{17,18},{19... | collective-permute-start | bytes 122888 | tf_op jit(solution)/shard_map/ppermute | solution.py:355
